TPU v7x, 32 devices: a whole 2x2x4 slice. The times are simulated.
32 devices in a mesh: dp: 8 (over y, x, core), head: 4 (over z).
Axes of the slice: x: 2, y: 2, z: 4, core: 2. Of those that a mesh axis runs over, the one named last changes fastest.
Arguments:
- tokens_in: bfloat16 [16384, 768], P(('dp', 'head')), may hold values from -6 to 6
- gain_attn: float32 [768], replicated, may hold values from 0.1 to 1.9
- gain_ffn: float32 [768], replicated, may hold values from 0.1 to 1.9
- w_qkv: bfloat16 [3, 768, 768], P(None, None, 'head'), may hold values from -0.3125 to 0.3125
- w_out: bfloat16 [768, 768], P('head'), may hold values from -0.5 to 0.5
- w_up: bfloat16 [768, 768], replicated, may hold values from -0.21875 to 0.21875
- w_down: bfloat16 [768, 768], replicated, may hold values from -0.21875 to 0.21875
- slot_mol: int32 [8, 16], P('dp'), may hold values from 0 to 11, never falling along the last dimension, each value on 1 to 2 neighbouring positions
- slot_fill: int32 [8, 16], P('dp'), may hold values from 16 to 128
- cotangent: bfloat16 [16384, 768], P(('dp', 'head')), may hold values from -6 to 6
Outputs:
- layer_out: bfloat16 [16384, 768], P(('dp', 'head'))
- d_tokens: float32 [16384, 768], P(('dp', 'head'))
- d_gain_attn: float32 [768], replicated
- d_gain_ffn: float32 [768], replicated
- d_w_qkv: float32 [3, 768, 768], P(None, None, 'head')
- d_w_out: float32 [768, 768], P('head')
- d_w_up: float32 [768, 768], replicated
- d_w_down: float32 [768, 768], replicated
Inputs may be any that keep to these rules, and one draw needn't show every extreme that they name: `slot_mol`: each group holds 12 molecules numbered in slot order; a molecule takes one slot or two consecutive slots. `slot_fill`: the live tokens of a slot are its first rows.
All inputs are finite; a program needn't handle non-finite values.
Results may differ from a plain program's by a relative error of at most 0.015.
The roundings to bfloat16 on the way count: a program that leaves them out, or rounds other values in their place, can miss the bound.
Values may be sent and summed in bfloat16 or wider, within the bound.
A program may use at most 128 MiB of HBM per device.

v0:
```python
import jax
import jax.numpy as jnp
from jax import lax
from jax.sharding import PartitionSpec as P

HEAD_DIM = 24
SLOT_LEN = 128


epsilon = 1e-05
masked_score = -1000000000.0


def layer_norm(values, scale_gain):
    row_mean = jnp.mean(values, axis=-1, keepdims=True)
    centred = values - row_mean
    variance = jnp.mean(centred * centred, axis=-1, keepdims=True)
    return centred * lax.rsqrt(variance + epsilon) * scale_gain


def gelu_exact(values):
    return jax.nn.gelu(values, approximate=False)


def local(
    tokens_in, gain_attn, gain_ffn, w_qkv, w_out, w_up, w_down, slot_mol, slot_fill, cotangent
):
    rows_dev = tokens_in.shape[0]
    head_count = lax.axis_size("head")
    group_rows = rows_dev * head_count
    local_width = w_out.shape[0]
    local_heads = local_width // HEAD_DIM
    query_scale = HEAD_DIM ** (-0.5)
    block_rows = min(512, group_rows)
    block_count = group_rows // block_rows
    key_window = block_rows + 2 * SLOT_LEN
    padded_rows = group_rows + 2 * SLOT_LEN
    mol_rows = jnp.repeat(slot_mol[0], SLOT_LEN)
    fill_rows = jnp.repeat(slot_fill[0], SLOT_LEN)
    live_rows = jnp.arange(group_rows, dtype=jnp.int32) % SLOT_LEN < fill_rows
    mol_keys = jnp.pad(mol_rows, SLOT_LEN, constant_values=-1)
    live_keys = jnp.pad(live_rows, SLOT_LEN, constant_values=False)
    input_float = tokens_in.astype(jnp.float32)
    normed, norm_back = jax.vjp(layer_norm, input_float, gain_attn)
    normed_low = normed.astype(jnp.bfloat16)
    gathered = lax.all_gather(normed_low, "head", axis=0, tiled=True)
    column_scale = jnp.array([query_scale, 1.0, 1.0], jnp.float32)[:, None, None]
    projected = jnp.einsum("td,cde->cte", gathered, w_qkv, preferred_element_type=jnp.float32)
    projected_low = (projected * column_scale).astype(jnp.bfloat16)
    queries = projected_low[0].reshape(group_rows, local_heads, HEAD_DIM)
    pad_rows = ((SLOT_LEN, SLOT_LEN), (0, 0))
    keys_pad = jnp.pad(projected_low[1], pad_rows).reshape(padded_rows, local_heads, HEAD_DIM)
    values_pad = jnp.pad(projected_low[2], pad_rows).reshape(padded_rows, local_heads, HEAD_DIM)

    def scores_of(first_row):
        query_block = lax.dynamic_slice_in_dim(queries, first_row, block_rows, 0)
        key_block = lax.dynamic_slice_in_dim(keys_pad, first_row, key_window, 0)
        mol_block = lax.dynamic_slice_in_dim(mol_rows, first_row, block_rows, 0)
        mol_window = lax.dynamic_slice_in_dim(mol_keys, first_row, key_window, 0)
        live_window = lax.dynamic_slice_in_dim(live_keys, first_row, key_window, 0)
        allowed = (mol_block[:, None] == mol_window[None, :]) & live_window[None, :]
        raw_scores = jnp.einsum(
            "qhe,khe->hqk", query_block, key_block, preferred_element_type=jnp.float32
        )
        return jnp.where(allowed[None], raw_scores, masked_score)

    def attend(block_index):
        first_row = block_index * block_rows
        scores = scores_of(first_row)
        row_max = jnp.max(scores, axis=-1, keepdims=True)
        exp_scores = jnp.exp(scores - row_max)
        row_sum = jnp.sum(exp_scores, axis=-1, keepdims=True)
        probs_low = (exp_scores / row_sum).astype(jnp.bfloat16)
        value_block = lax.dynamic_slice_in_dim(values_pad, first_row, key_window, 0)
        mixed_block = jnp.einsum(
            "hqk,khe->qhe", probs_low, value_block, preferred_element_type=jnp.float32
        )
        return (
            mixed_block.reshape(block_rows, local_width).astype(jnp.bfloat16),
            (row_max + jnp.log(row_sum))[..., 0],
        )

    mixed_heads, log_sums = lax.map(attend, jnp.arange(block_count, dtype=jnp.int32))
    mixed_heads = mixed_heads.reshape(group_rows, local_width)
    mixed_rows = mixed_heads
    branch = lax.psum_scatter(
        jnp.dot(mixed_rows, w_out, preferred_element_type=jnp.float32),
        "head",
        scatter_dimension=0,
        tiled=True,
    )
    residual = input_float + branch
    normed_ffn, norm_ffn_back = jax.vjp(layer_norm, residual, gain_ffn)
    normed_ffn_low = normed_ffn.astype(jnp.bfloat16)
    ffn_inner = jnp.dot(normed_ffn_low, w_up, preferred_element_type=jnp.float32)
    activated, gelu_back = jax.vjp(gelu_exact, ffn_inner)
    hidden = activated.astype(jnp.bfloat16)
    output = (residual + jnp.dot(hidden, w_down, preferred_element_type=jnp.float32)).astype(
        jnp.bfloat16
    )
    grad_down = jnp.einsum("rf,rd->fd", hidden, cotangent, preferred_element_type=jnp.float32)
    d_hidden = jnp.einsum("rd,fd->rf", cotangent, w_down, preferred_element_type=jnp.float32)
    d_inner = gelu_back(d_hidden)[0].astype(jnp.bfloat16)
    grad_up = jnp.einsum("rd,rf->df", normed_ffn_low, d_inner, preferred_element_type=jnp.float32)
    d_normed_ffn = jnp.einsum("rf,df->rd", d_inner, w_up, preferred_element_type=jnp.float32)
    d_residual_norm, grad_gain_ffn = norm_ffn_back(d_normed_ffn)
    d_residual = cotangent.astype(jnp.float32) + d_residual_norm
    d_branch = d_residual.astype(jnp.bfloat16)
    shard_rows = lax.all_gather(d_branch, "head", axis=0, tiled=True)
    mixed_rows = mixed_heads
    grad_acc = jnp.einsum("te,td->ed", mixed_rows, shard_rows, preferred_element_type=jnp.float32)
    d_rows = jnp.einsum("td,ed->te", shard_rows, w_out, preferred_element_type=jnp.float32)
    grad_out = grad_acc
    d_mixed_low = d_rows.astype(jnp.bfloat16).reshape(group_rows, local_heads, HEAD_DIM)

    def back_block(running, block_index):
        d_key_acc, d_value_acc = running
        first_row = block_index * block_rows
        scores = scores_of(first_row)
        attn_probs = jnp.exp(scores - log_sums[block_index][:, :, None])
        probs_low = attn_probs.astype(jnp.bfloat16)
        query_block = lax.dynamic_slice_in_dim(queries, first_row, block_rows, 0)
        key_block = lax.dynamic_slice_in_dim(keys_pad, first_row, key_window, 0)
        value_block = lax.dynamic_slice_in_dim(values_pad, first_row, key_window, 0)
        grad_block = lax.dynamic_slice_in_dim(d_mixed_low, first_row, block_rows, 0)
        d_probs = jnp.einsum(
            "qhe,khe->hqk", grad_block, value_block, preferred_element_type=jnp.float32
        )
        inner_sum = jnp.sum(attn_probs * d_probs, axis=-1, keepdims=True)
        d_scores = (attn_probs * (d_probs - inner_sum)).astype(jnp.bfloat16)
        d_query = query_scale * jnp.einsum(
            "hqk,khe->qhe", d_scores, key_block, preferred_element_type=jnp.float32
        )
        d_key_block = jnp.einsum(
            "hqk,qhe->khe", d_scores, query_block, preferred_element_type=jnp.float32
        )
        d_value_block = jnp.einsum(
            "hqk,qhe->khe", probs_low, grad_block, preferred_element_type=jnp.float32
        )
        key_part = lax.dynamic_slice_in_dim(d_key_acc, first_row, key_window, 0)
        d_key_acc = lax.dynamic_update_slice_in_dim(d_key_acc, key_part + d_key_block, first_row, 0)
        value_part = lax.dynamic_slice_in_dim(d_value_acc, first_row, key_window, 0)
        d_value_acc = lax.dynamic_update_slice_in_dim(
            d_value_acc, value_part + d_value_block, first_row, 0
        )
        return ((d_key_acc, d_value_acc), d_query.astype(jnp.bfloat16))

    zero_pad = jnp.zeros((padded_rows, local_heads, HEAD_DIM), jnp.float32)
    (d_key_acc, d_value_acc), d_query = lax.scan(
        back_block, (zero_pad, zero_pad), jnp.arange(block_count, dtype=jnp.int32)
    )
    d_query = d_query.reshape(group_rows, local_width)
    d_key = (
        d_key_acc[SLOT_LEN : SLOT_LEN + group_rows]
        .reshape(group_rows, local_width)
        .astype(jnp.bfloat16)
    )
    d_value = (
        d_value_acc[SLOT_LEN : SLOT_LEN + group_rows]
        .reshape(group_rows, local_width)
        .astype(jnp.bfloat16)
    )
    d_qkv = jnp.stack([d_query, d_key, d_value])
    grad_qkv = jnp.einsum("td,cte->cde", gathered, d_qkv, preferred_element_type=jnp.float32)
    d_normed = lax.psum_scatter(
        jnp.einsum("cte,cde->td", d_qkv, w_qkv, preferred_element_type=jnp.float32).astype(
            jnp.bfloat16
        ),
        "head",
        scatter_dimension=0,
        tiled=True,
    ).astype(jnp.float32)
    d_input_norm, grad_gain_attn = norm_back(d_normed)
    d_tokens = d_residual + d_input_norm
    grad_qkv, grad_out = lax.psum((grad_qkv, grad_out), "dp")
    grad_up, grad_down, grad_gain_attn, grad_gain_ffn = lax.psum(
        (grad_up, grad_down, grad_gain_attn, grad_gain_ffn), ("dp", "head")
    )
    return (output, d_tokens, grad_gain_attn, grad_gain_ffn, grad_qkv, grad_out, grad_up, grad_down)


def solution(mesh):
    return jax.shard_map(
        local,
        mesh=mesh,
        in_specs=(
            P(("dp", "head"), None),
            P(),
            P(),
            P(None, None, "head"),
            P("head", None),
            P(),
            P(),
            P("dp", None),
            P("dp", None),
            P(("dp", "head"), None),
        ),
        out_specs=(
            P(("dp", "head"), None),
            P(("dp", "head"), None),
            P(),
            P(),
            P(None, None, "head"),
            P("head", None),
            P(),
            P(),
        ),
        check_vma=False,
    )
```

profile of v0, /device:TPU:0, one launch (start us, length us, event | category | flops | bytes accessed | tf_op | source)
XLA Modules:
  0.0 744.3 jit_solution(16228574355169517621)
XLA Ops:
  13.0 66.1 %all-gather.3.cloned.1.call-done = bf16[2048,768]{1,0:T(8,128)(2,1)} async-done(((bf16[512,768]{1,0:T(8,128)(2,1)}), bf16[2048,768]{1,0:T(8,128)(2,1)}) %all-gather.3.cloned.1.call-update) | async-done | bytes 3145744 | tf_op jit(solution)/shard_map/all_gather | solution.py:46
  79.0 3.9 fusion.80
  85.8 52.1 %while.26 = (s32[]{:T(128)}, bf16[4,512,192]{1,2,0:T(8,128)(2,1)}, f32[4,8,512]{2,1,0:T(8,128)S(1)}, s32[4]{0:T(128)S(1)}, bf16[2304,8,24]{0,2,1:T(8,128)(2,1)},...) while((s32[]{:T(128)}, bf16[4,512,192]{1,2,0:T(8,128)(2,1)}, ...), condition=%wide.region_5.6_spmd, body=%wide.region_2.5_spmd.sunk | while | flops 331182080 | bytes 40846856 | solution.py:83
  87.6 3.0 select_reduce_fusion.2
  90.6 3.0 fusion.121
  93.6 4.5 fusion.122
  100.6 3.0 select_reduce_fusion.2
  103.6 3.0 fusion.121
  106.6 4.5 fusion.122
  113.6 3.0 select_reduce_fusion.2
  116.6 3.0 fusion.121
  119.6 4.5 fusion.122
  126.6 3.0 select_reduce_fusion.2
  129.6 3.0 fusion.121
  132.7 4.5 fusion.122
  140.0 3.7 fusion.81
  143.9 109.4 %reduce-scatter.3.cloned.1.call-done = f32[512,768]{1,0:T(8,128)} async-done(((f32[2048,768]{1,0:T(8,128)}), f32[512,768]{1,0:T(8,128)}) %reduce-scatter.3.cloned.1.call-update) | async-done | bytes 1572880 | tf_op jit(solution)/shard_map/reduce_scatter | solution.py:86
  257.9 5.1 add_convert_fusion
  267.7 64.0 %all-gather.5.cloned.1.call-done = bf16[2048,768]{1,0:T(8,128)(2,1)} async-done(((bf16[512,768]{1,0:T(8,128)(2,1)}), bf16[2048,768]{1,0:T(8,128)(2,1)}) %all-gather.5.cloned.1.call-update) | async-done | bytes 3145744 | tf_op jit(solution)/shard_map/all_gather | solution.py:109
  331.7 3.1 convolution_convert_fusion
  337.4 104.5 %while.27 = (s32[]{:T(128)}, f32[2304,8,24]{0,2,1:T(8,128)}, f32[2304,8,24]{0,2,1:T(8,128)}, bf16[4,512,8,24]{1,3,2,0:T(8,128)(2,1)}, s32[4]{0:T(128)S(1)}, /*in...) while((s32[]{:T(128)}, f32[2304,8,24]{0,2,1:T(8,128)}, ...), condition=%wide.region_13.14_spmd, body=%wide.region_11.13_spmd.sunk | while | flops 793997312 | bytes 113673928 | solution.py:149
  344.1 4.5 fusion.133
  348.5 5.3 multiply_reduce_fusion.5
  353.9 3.2 multiply_convert_fusion.7
  357.1 3.4 fusion.134
  360.5 3.1 fusion.132
  370.2 4.5 fusion.133
  374.7 5.3 multiply_reduce_fusion.5
  380.0 3.2 multiply_convert_fusion.7
  383.2 3.4 fusion.134
  386.6 3.1 fusion.132
  396.3 4.5 fusion.133
  400.8 5.3 multiply_reduce_fusion.5
  406.1 3.2 multiply_convert_fusion.7
  409.3 3.4 fusion.134
  412.7 3.1 fusion.132
  422.4 4.5 fusion.133
  426.9 5.3 multiply_reduce_fusion.5
  432.2 3.2 multiply_convert_fusion.7
  435.5 3.4 fusion.134
  438.9 3.1 fusion.132
  448.8 4.1 bitcast_convert_fusion
  465.7 5.1 fusion.62
  470.8 41.3 %reduce-scatter.5.cloned.1.call-done = bf16[512,768]{1,0:T(8,128)(2,1)} async-done(((bf16[2048,768]{1,0:T(8,128)(2,1)}), bf16[512,768]{1,0:T(8,128)(2,1)}) %reduce-scatter.5.cloned.1.call-update) | async-done | bytes 786448 | tf_op jit(solution)/shard_map/reduce_scatter | solution.py:165
  517.1 40.9 %all-reduce.4 = (f32[768]{0:T(1024)}, f32[768]{0:T(1024)}) all-reduce(f32[768]{0:T(1024)} %get-tuple-element.137, f32[768]{0:T(1024)} %get-tuple-element.135), channel_id=1, replica_groups=mesh['dp'=8,'head'=4] {'dp','head'}, use_global_device_ids=true, to_apply=%region_18.19 | all-reduce | flops 1536 | bytes 12288 | tf_op jit(solution)/shard_map/psum | solution.py:176
  558.7 3.4 add_add_fusion.2
  562.1 102.0 %all-reduce.10.cloned.1.call-done = (f32[768,768]{1,0:T(8,128)}, f32[768,768]{1,0:T(8,128)}) async-done(((f32[768,768]{1,0:T(8,128)}, f32[768,768]{1,0:T(8,128)}), (f32[768,768]{1,0:T(8,128)}, f32[768,768]{1,0:T(8,128)})) %all-reduce.10.cloned.1.call-update) | async-done | bytes 4718608 | tf_op jit(solution)/shard_map/psum | solution.py:176
  664.1 65.6 %all-reduce.12.cloned.1.call-done = (f32[3,768,192]{1,2,0:T(8,128)}, f32[192,768]{1,0:T(8,128)}) async-done(((f32[3,768,192]{1,2,0:T(8,128)}, f32[192,768]{1,0:T(8,128)}), (f32[3,768,192]{1,2,0:T(8,128)}, f32[192,768]{1,0:T(8,128)})) %all-reduce.12.cloned.1.call-update) | async-done | bytes 2359312 | tf_op jit(solution)/shard_map/psum | solution.py:175
  (242 shorter events, 79.2 us)
Async XLA Ops:
  7.2 250.5 %copy-start = (bf16[768,768]{1,0:T(8,128)(2,1)S(1)}, bf16[768,768]{1,0:T(8,128)(2,1)}, u32[]{:S(2)}) copy-start(bf16[768,768]{1,0:T(8,128)(2,1)} %param.21) | copy-start | bytes 3538948
  7.2 4.3 copy-start.1
  7.2 4.3 copy-start.33
  7.2 71.8 %all-gather.3.cloned.1.call-start = ((), (), s32[]{:S(2)}) async-start(), calls=%async_computation.2 | async-start | bytes 3932160 | tf_op jit(solution)/shard_map/all_gather | solution.py:46
  8.7 4.1 copy-start.46
  8.7 4.2 copy-start.47
  8.7 70.3 %copy-start.49 = (bf16[3,768,192]{1,2,0:T(8,128)(2,1)S(1)}, bf16[3,768,192]{1,2,0:T(8,128)(2,1)}, u32[]{:S(2)}) copy-start(bf16[3,768,192]{1,2,0:T(8,128)(2,1)} %param.18) | copy-start | bytes 2654212
  12.7 240.6 %reduce-scatter.3.cloned.1.call-start = ((), (), s32[]{:S(2)}) async-start(), calls=%async_computation.3 | async-start | bytes 7864320 | tf_op jit(solution)/shard_map/reduce_scatter | solution.py:86
  79.0 3.9 copy-start.45
  143.7 188.0 %all-gather.5.cloned.1.call-start = ((), (), s32[]{:S(2)}) async-start(), calls=%async_computation.4 | async-start | bytes 3932160 | tf_op jit(solution)/shard_map/all_gather | solution.py:109
  254.9 9.7 %copy-start.5 = (f32[512,768]{1,0:T(8,128)}, f32[512,768]{1,0:T(8,128)S(1)}, u32[]{:S(2)}) copy-start(f32[512,768]{1,0:T(8,128)S(1)} %get-tuple-element.196) | copy-start | bytes 4718596
  255.0 9.6 %copy-start.37 = (f32[512]{0:T(512)}, f32[512]{0:T(512)S(1)}, u32[]{:S(2)}) copy-start(f32[512]{0:T(512)S(1)} %broadcast_multiply_fusion) | copy-start | bytes 6148
  256.8 7.8 %copy-start.39 = (f32[512]{0:T(512)}, f32[512]{0:T(512)S(1)}, u32[]{:S(2)}) copy-start(f32[512]{0:T(512)S(1)} %fusion.72) | copy-start | bytes 6148
  257.9 5.1 copy-start.19
  267.6 244.6 %reduce-scatter.5.cloned.1.call-start = ((), (), s32[]{:S(2)}) async-start(), calls=%async_computation.5 | async-start | bytes 3932160 | tf_op jit(solution)/shard_map/reduce_scatter | solution.py:165
  337.4 6.6 copy-start.3
  337.4 6.6 copy-start.14
  360.5 3.1 copy-start.4
  360.5 3.1 copy-start.15
  363.6 6.6 copy-start.3
  363.6 6.6 copy-start.14
  386.6 3.1 copy-start.4
  386.6 3.1 copy-start.15
  389.7 6.6 copy-start.3
  389.7 6.6 copy-start.14
  412.7 3.1 copy-start.4
  412.7 3.1 copy-start.15
  415.8 6.6 copy-start.3
  415.8 6.6 copy-start.14
  438.9 3.1 copy-start.4
  438.9 3.1 copy-start.15
  444.3 3.6 copy-start.23
  444.3 4.6 copy-start.50
  453.0 211.2 %all-reduce.10.cloned.1.call-start = ((), (), s32[]{:S(2)}) async-start(), calls=%async_computation.6 | async-start | bytes 9437184 | tf_op jit(solution)/shard_map/psum | solution.py:176
  456.1 2.5 copy-start.22
  456.1 2.5 copy-start.38
  456.1 2.5 copy-start.40
  461.0 3.0 copy-start.10
  461.0 268.8 %all-reduce.12.cloned.1.call-start = ((), (), s32[]{:S(2)}) async-start(), calls=%async_computation.7 | async-start | bytes 4718592 | tf_op jit(solution)/shard_map/psum | solution.py:175
  461.0 3.0 copy-start.16
  470.8 41.4 %copy-start.2 = (bf16[512,768]{1,0:T(8,128)(2,1)S(1)}, bf16[512,768]{1,0:T(8,128)(2,1)}, u32[]{:S(2)}) copy-start(bf16[512,768]{1,0:T(8,128)(2,1)} %param.15) | copy-start | bytes 2359300
  470.8 41.4 %copy-start.32 = (f32[512]{0:T(512)S(1)}, f32[512]{0:T(512)}, u32[]{:S(2)}) copy-start(f32[512]{0:T(512)} %copy-done.31) | copy-start | bytes 6148
  470.8 41.4 %copy-start.34 = (f32[768]{0:T(1024)S(1)}, f32[768]{0:T(1024)}, u32[]{:S(2)}) copy-start(f32[768]{0:T(1024)} %param.16) | copy-start | bytes 9220
  470.8 43.7 %copy-start.36 = (f32[512]{0:T(512)S(1)}, f32[512]{0:T(512)}, u32[]{:S(2)}) copy-start(f32[512]{0:T(512)} %copy-done.35) | copy-start | bytes 6148
  470.8 87.9 %copy-start.8 = (f32[512,768]{1,0:T(8,128)S(1)}, f32[512,768]{1,0:T(8,128)}, u32[]{:S(2)}) copy-start(f32[512,768]{1,0:T(8,128)} %copy-done.7) | copy-start | bytes 4718596
  729.8 3.0 copy-start.29
  729.8 3.8 copy-start.18
  733.5 2.5 copy-start.17
  (21 other events, 32.0 us)
Sparse Core Ops, SparseCore 0:
  12.8 66.1 all-gather.2
  143.8 109.4 reduce-scatter.2
  267.7 63.9 all-gather.4
  453.1 59.0 reduce-scatter.4
  518.4 145.6 all-reduce.9
  667.9 61.8 all-reduce.11
where the time goes:
time: 746 us; the launch traced here: 744 us
  waiting for transfers between devices  449 us (60%)
  matrix products  143 us (19%)
  other arithmetic  46.8 us (6%)
  blocking collectives  40.9 us (5%)
  local copies, waits for them, and re-layouts  37.4 us (5%)
  between operations  14.6 us (2%)
  loops' own time  13.1 us (2%)
    reduce_scatter x1, waiting for transfers between devices, local(): lax.psum_scatter(jnp.dot(mixed_rows, w_out, preferred_element_type=jnp.fl...  109 us
    psum x1, waiting for transfers between devices, local(): lax.psum((grad_up, grad_down, grad_gain_attn, grad_gain_ffn), ('dp', 'hea...  102 us
    all_gather x1, waiting for transfers between devices, local(): gathered = lax.all_gather(normed_low, 'head', axis=0, tiled=True)  66.1 us
    psum x1, waiting for transfers between devices, local(): grad_qkv, grad_out = lax.psum((grad_qkv, grad_out), 'dp')  65.6 us
    all_gather x1, waiting for transfers between devices, local(): shard_rows = lax.all_gather(d_branch, 'head', axis=0, tiled=True)  64 us
    reduce_scatter x1, waiting for transfers between devices, local(): lax.psum_scatter(jnp.einsum('cte,cde->td', d_qkv, w_qkv, preferred_elemen...  41.3 us
    psum x1, blocking collectives, local(): lax.psum((grad_up, grad_down, grad_gain_attn, grad_gain_ffn), ('dp', 'hea...  40.9 us
    dot_general x8, matrix products, scores_of(): jnp.einsum('qhe,khe->hqk', query_block, key_block, preferred_element_type...  23.2 us
  transfers between devices with their start and end apart: 6, of which 6 were waited for; matrix products, arithmetic and copies ran while one was open for 3% of the time, Pallas kernels for 0%

commit v1 on v0

v1 whole, which is shorter than its diff:
```python
import functools

import jax
import jax.numpy as jnp
from jax import lax
from jax.experimental import pallas as pl
from jax.experimental.pallas import tpu as pltpu
from jax.sharding import PartitionSpec as P

HEAD_DIM = 24
SLOT = 128
D = 768
EPS = 1e-05
SLOTS_DEV = 4
ROWS = SLOTS_DEV * SLOT
WIN = ROWS + 2 * SLOT
BF = jnp.bfloat16
F32 = jnp.float32


def nn(a, b):
    return jnp.dot(a, b, preferred_element_type=F32)


def nt(a, b):
    return lax.dot_general(a, b, (((1,), (1,)), ((), ())), preferred_element_type=F32)


def tn(a, b):
    return lax.dot_general(a, b, (((0,), (0,)), ((), ())), preferred_element_type=F32)


def norm_stats(v):
    mean = jnp.mean(v, axis=-1, keepdims=True)
    centred = v - mean
    var = jnp.mean(centred * centred, axis=-1, keepdims=True)
    r = lax.rsqrt(var + EPS)
    return centred * r, r


def norm_back(grad, z, r, gain):
    e = grad * gain
    return r * (e - jnp.mean(e, -1, keepdims=True) - z * jnp.mean(e * z, -1, keepdims=True))


def build_masks(mask_ref, width):
    rows = lax.broadcasted_iota(jnp.int32, (width, 2 * SLOT), 0)
    right = (lax.broadcasted_iota(jnp.int32, (width, 2 * SLOT), 1) >= SLOT).astype(jnp.int32)
    for p in range(mask_ref.shape[0]):
        low = (2 * p + right) * HEAD_DIM
        keep = (rows >= low) & (rows < low + HEAD_DIM)
        mask_ref[p] = jnp.where(keep, 1.0, 0.0).astype(BF)


def slot_meta(mol_ref, fill_ref, z, s):
    at = z * SLOTS_DEV + s
    last = mol_ref.shape[1] - 1
    before, after = jnp.maximum(at - 1, 0), jnp.minimum(at + 1, last)
    mine = mol_ref[0, at]
    prev = jnp.where((mol_ref[0, before] == mine) & (at > 0), 1, 0)
    nxt = jnp.where((mol_ref[0, after] == mine) & (at < last), 1, 0)
    partner = prev * fill_ref[0, before] + nxt * fill_ref[0, after]
    return prev, nxt, fill_ref[0, at], partner


def key_bias(own, partner):
    at = lax.broadcasted_iota(jnp.int32, (SLOT, SLOT), 0)
    top = jnp.where(at < own, 0.0, -1e30).astype(F32)
    low = jnp.where(at < partner, 0.0, -1e30).astype(F32)
    one = jnp.concatenate([top, low], axis=0)
    return jnp.concatenate([one, one], axis=1)


def pick(flag, a, b):
    keep = jnp.broadcast_to(flag, a.shape) == 1
    return jnp.where(keep, a.astype(F32), b.astype(F32)).astype(a.dtype)


def pair_rows(full):
    rows = lax.broadcasted_iota(jnp.int32, (2 * HEAD_DIM, SLOT), 0)
    return jnp.where(rows < HEAD_DIM, full[:, :SLOT], full[:, SLOT:])


def project(g, parts, nw, qt, kt, vt, kn, vn, scale):
    own = nw[pl.ds(SLOT, ROWS), :]
    qt[g] = (nt(parts[0], own) * scale).astype(BF)
    k = nt(parts[1], nw[...]).astype(BF)
    kt[g] = k
    kn[g] = k.T
    v = nt(parts[2], nw[...]).astype(BF)
    vt[g] = v
    vn[g] = v.T


def windows(s):
    own = pl.multiple_of((s + 1) * SLOT, SLOT)
    before = pl.multiple_of(s * SLOT, SLOT)
    after = pl.multiple_of((s + 2) * SLOT, SLOT)
    return pl.ds(own, SLOT), pl.ds(before, SLOT), pl.ds(after, SLOT), pl.ds(before, SLOT)


def attend(g, s, meta, mask, qt, kn, vt, probs, mixf, mixt):
    prev, _, own_live, partner_live = meta
    own, before, after, mine = windows(s)
    width = qt.shape[1]
    pairs = mask.shape[0]
    keys = jnp.concatenate([kn[g, own, :], pick(prev, kn[g, before, :], kn[g, after, :])], axis=0)
    vals = jnp.concatenate([vt[g, :, own], pick(prev, vt[g, :, before], vt[g, :, after])], axis=1)
    q = qt[g, :, mine]
    q2 = jnp.concatenate([q, q], axis=1)
    bias = key_bias(own_live, partner_live)
    for p in range(pairs):
        scores = nn(keys, q2 * mask[p]) + bias
        top = jnp.max(scores, axis=0, keepdims=True)
        ex = jnp.exp(scores - top)
        total = jnp.sum(ex, axis=0, keepdims=True)
        pr = (ex * (1.0 / total)).astype(BF)
        probs[g, s, p] = pr
        head_rows = slice(2 * HEAD_DIM * p, 2 * HEAD_DIM * (p + 1))
        mixed = pair_rows(nn(vals[head_rows, :], pr))
        mixf[g, head_rows, mine] = mixed
        at = pl.ds(pl.multiple_of(g * width + 2 * HEAD_DIM * p, 16), 2 * HEAD_DIM)
        mixt[at, mine] = mixed.astype(BF)


def attend_back(g, s, meta, mask, qt, kt, vn, dmt, probs, mixf, dqkv, dkt, dvt, scale):
    prev, nxt, _, _ = meta
    own, before, after, mine = windows(s)
    pairs = mask.shape[0]
    fprev, fnext = prev.astype(F32), nxt.astype(F32)
    vals = jnp.concatenate([vn[g, own, :], pick(prev, vn[g, before, :], vn[g, after, :])], axis=0)
    keys = jnp.concatenate([kt[g, :, own], pick(prev, kt[g, :, before], kt[g, :, after])], axis=1)
    q = qt[g, :, mine]
    dm = dmt[g, :, mine]
    q2 = jnp.concatenate([q, q], axis=1)
    dm2 = jnp.concatenate([dm, dm], axis=1)
    prod = dm.astype(F32) * mixf[g, :, mine]
    for p in range(pairs):
        head_rows = slice(2 * HEAD_DIM * p, 2 * HEAD_DIM * (p + 1))
        mid = 2 * HEAD_DIM * p + HEAD_DIM
        inner = jnp.concatenate(
            [
                jnp.sum(prod[2 * HEAD_DIM * p : mid], axis=0, keepdims=True),
                jnp.sum(prod[mid : mid + HEAD_DIM], axis=0, keepdims=True),
            ],
            axis=1,
        )
        rhs = dm2 * mask[p]
        d_probs = nn(vals, rhs)
        pr = probs[g, s, p]
        d_scores = (pr.astype(F32) * (d_probs - inner)).astype(BF)
        dq = pair_rows(nn(keys[head_rows, :], d_scores)) * scale
        dqkv[g, 0, head_rows, mine] = dq.astype(BF)
        qm = (q2 * mask[p])[head_rows, :]
        dk = nt(qm, d_scores)
        dv = nt(rhs[head_rows, :], pr)
        dkt[g, head_rows, own] += dk[:, :SLOT]
        dvt[g, head_rows, own] += dv[:, :SLOT]
        dkt[g, head_rows, before] += fprev * dk[:, SLOT:]
        dvt[g, head_rows, before] += fprev * dv[:, SLOT:]
        dkt[g, head_rows, after] += fnext * dk[:, SLOT:]
        dvt[g, head_rows, after] += fnext * dv[:, SLOT:]


SQH = 0.7071067811865476
PHI = 0.3989422804014327
MESH = pl.DeviceIdType.MESH
HALVINGS = 3
PIECE = D // 8
LANE = PIECE // 2


class Link:
    def __init__(self, send_sem, recv_sem):
        self.send_sem, self.recv_sem, self.used, self.open = send_sem, recv_sem, 0, []

    def make(self, src, dst, target):
        slot = self.used
        self.used += 1
        return pltpu.make_async_remote_copy(
            src_ref=src, dst_ref=dst, send_sem=self.send_sem.at[slot], recv_sem=self.recv_sem.at[slot],
            device_id=target, device_id_type=MESH,
        )

    def send(self, src, dst, target):
        copy = self.make(src, dst, target)
        copy.start()
        self.open.append(copy)
        return copy

    def done(self, copy):
        copy.wait_send()
        self.open = [c for c in self.open if c is not copy]

    def drain(self):
        for copy in self.open:
            copy.wait_send()
        self.open = []


def add_rows(dst, *terms):
    if len(dst.shape) == 3:
        for unit in range(dst.shape[0]):
            add_rows(dst.at[unit], *[term.at[unit] for term in terms])
        return

    @pl.loop(0, dst.shape[0] // 16)
    def _(i):
        at = pl.ds(pl.multiple_of(i * 16, 16), 16)
        total = dst[at, :].astype(F32)
        for term in terms:
            total = total + term[at, :].astype(F32)
        dst[at, :] = total.astype(dst.dtype)


def piece_rows(d0, d1, d2, lane):
    return pl.ds(pl.multiple_of(((d0 * 2 + d1) * 2 + d2) * PIECE + lane * LANE, 16), LANE)


def half_rows(d0):
    return pl.ds(pl.multiple_of(d0 * (D // 2), 16), D // 2)


def take(ref, rows):
    return ref.at[:, rows] if len(ref.shape) == 3 else ref.at[rows]


class Place:
    def __init__(self, dp_size, shards):
        self.dp = lax.axis_index("dp")
        self.z = lax.axis_index("head")
        self.shards = shards
        self.bits, self.partner = [], []
        step = 1
        while step < dp_size:
            bit = (self.dp // step) % 2
            self.bits.append(bit)
            self.partner.append(self.dp + step - 2 * step * bit)
            step *= 2
        self.order = ((0, 1, 2), (0, 2, 1))

    def near(self, bit):
        return {"dp": self.partner[bit]}

    def across(self, k):
        step, found = 1, 0
        while step < self.shards:
            bit = (self.z // step) % 2
            found = found + step * ((bit + 1) % 2 if (k // step) % 2 else bit)
            step *= 2
        return found

    def index(self, lane):
        return tuple(self.bits[b] for b in self.order[lane])


class Halve:
    def __init__(self, link, place, g, r0, r1, r2, rx):
        self.link, self.place, self.g, self.r0, self.r1, self.r2, self.rx = link, place, g, r0, r1, r2, rx

    def start(self):
        c0 = self.place.bits[0]
        self.copies = [self.link.send(take(self.g, half_rows(1 - c0)), self.r0, self.place.near(0))]

    def mine(self, lane):
        return take(self.g, piece_rows(*self.place.index(lane), lane))

    def step1(self):
        p = self.place
        self.copies[0].wait_recv()
        self.copies = []
        for lane in range(2):
            c0, c1, _ = p.index(lane)
            sent = []
            for b in range(2):
                part = take(self.g, piece_rows(c0, 1 - c1, b, lane))
                add_rows(part, take(self.r0, piece_rows(0, 1 - c1, b, lane)))
                sent.append(self.link.send(part, self.r1.at[lane, b], p.near(p.order[lane][1])))
            self.copies.append(sent)
        for lane in range(2):
            c0, c1, _ = p.index(lane)
            for b in range(2):
                add_rows(take(self.g, piece_rows(c0, c1, b, lane)), take(self.r0, piece_rows(0, c1, b, lane)))

    def step2(self):
        p = self.place
        old, self.copies = self.copies, []
        for lane in range(2):
            c0, c1, c2 = p.index(lane)
            for copy in old[lane]:
                copy.wait_recv()
            part = take(self.g, piece_rows(c0, c1, 1 - c2, lane))
            add_rows(part, self.r1.at[lane, 1 - c2])
            self.copies.append(self.link.send(part, self.r2.at[lane], p.near(p.order[lane][2])))
        for lane in range(2):
            _, _, c2 = p.index(lane)
            add_rows(self.mine(lane), self.r1.at[lane, c2])

    def step3(self):
        p = self.place
        for lane in range(2):
            self.copies[lane].wait_recv()
            add_rows(self.mine(lane), self.r2.at[lane])
        for extra in range(HALVINGS, len(p.bits)):
            copies = [
                self.link.send(self.mine(lane), self.rx.at[extra - HALVINGS, lane], p.near(extra)) for lane in range(2)
            ]
            for lane in range(2):
                copies[lane].wait_recv()
                self.link.done(copies[lane])
                add_rows(self.mine(lane), self.rx.at[extra - HALVINGS, lane])


class Spread:
    def __init__(self, link, place, f):
        self.link, self.place, self.f = link, place, f

    def swap(self, rows, bit):
        part = take(self.f, rows)
        return self.link.send(part, part, self.place.near(bit))

    def start(self):
        p = self.place
        self.copies = [[self.swap(piece_rows(*p.index(lane), lane), p.order[lane][2])] for lane in range(2)]

    def step1(self):
        p = self.place
        old, self.copies = self.copies, []
        for lane in range(2):
            c0, c1, _ = p.index(lane)
            for copy in old[lane]:
                copy.wait_recv()
            self.copies.append([self.swap(piece_rows(c0, c1, b, lane), p.order[lane][1]) for b in range(2)])

    def step2(self):
        for lane in range(2):
            for copy in self.copies[lane]:
                copy.wait_recv()
        self.copies = [self.swap(half_rows(self.place.bits[0]), 0)]

    def finish(self):
        self.copies[0].wait_recv()


def kernel(
    dp_size, shards,
    mol, fill, x, cot, gain_a, gain_f, wown, wu, wd,
    out, dtok, gains_out, f_ud, f_own,
    wg, nw, xh, mask, qt, kt, vt, kn, vn, probs, mixf, mixt, dmt, dbr, dres,
    dqkv, dkt, dvt, halo_out, halo_in, g_ud, g_k, r0u, r1u, r2u, rxu, r0, r1, r2, rx, zud, zk,
    gain_sum, gain_got, gain_col,
    send_sem, recv_sem, halo_send, halo_recv, load_sem,
):
    place = Place(dp_size, shards)
    link = Link(send_sem, recv_sem)
    z = place.z
    last = shards - 1
    nffn, hidden, dinner = (g_k.at[i, pl.ds(0, ROWS)] for i in range(3))
    scale = HEAD_DIM ** (-0.5)
    width = qt.shape[1]

    def column(k):
        return {"head": place.across(k)}

    barrier = pltpu.get_barrier_semaphore()
    peers = [place.near(b) for b in range(len(place.bits))] + [column(k) for k in range(1, shards)]
    for peer in peers:
        pl.semaphore_signal(barrier, inc=1, device_id=peer, device_id_type=MESH)
    pl.semaphore_wait(barrier, len(peers))

    own_w = pltpu.make_async_copy(wown, wg.at[z], load_sem)
    own_w.start()
    after = {"head": jnp.minimum(z + 1, last)}
    before = {"head": jnp.maximum(z - 1, 0)}
    to_next = link.make(x.at[pl.ds(ROWS - SLOT, SLOT)], xh.at[0], after)
    to_prev = link.make(x.at[pl.ds(0, SLOT)], xh.at[1], before)

    @pl.when(z < last)
    def _():
        to_next.start()

    @pl.when(z > 0)
    def _():
        to_prev.start()

    gather = []
    for k in range(1, shards):
        copies = []
        for lane in range(2):
            rows = piece_rows(*place.index(lane), lane)
            copies.append(link.send(wown.at[rows], wg.at[z, rows], column(k)))
        gather.append((copies, Spread(link, place, wg.at[place.across(k)])))

    build_masks(mask, width)

    def normed(at_w, ref, at):
        zz, _ = norm_stats(ref[at, :].astype(F32))
        nw[at_w, :] = (zz * gain_a[...]).astype(BF)

    @pl.loop(0, ROWS // 64)
    def _(i):
        at = pl.multiple_of(i * 64, 64)
        normed(pl.ds(at + SLOT, 64), x, pl.ds(at, 64))

    @pl.when(z > 0)
    def _():
        to_next.wait_recv()

    @pl.when(z == 0)
    def _():
        xh[0] = jnp.zeros_like(xh[0])

    @pl.when(z < last)
    def _():
        to_prev.wait_recv()

    @pl.when(z == last)
    def _():
        xh[1] = jnp.zeros_like(xh[1])

    @pl.loop(0, SLOT // 64)
    def _(i):
        at = pl.multiple_of(i * 64, 64)
        normed(pl.ds(at, 64), xh.at[0], pl.ds(at, 64))
        normed(pl.ds(at + SLOT + ROWS, 64), xh.at[1], pl.ds(at, 64))

    def weight(g, c):
        return wg[g, c * width : (c + 1) * width, :]

    def forward(g):
        project(g, [weight(g, c) for c in range(3)], nw, qt, kt, vt, kn, vn, scale)

        @pl.loop(0, SLOTS_DEV)
        def _(s):
            attend(g, s, slot_meta(mol, fill, z, s), mask, qt, kn, vt, probs, mixf, mixt)

    own_w.wait()
    forward(z)
    for copies, spread in gather:
        for copy in copies:
            copy.wait_recv()
        spread.start()
    for _, spread in gather:
        spread.step1()
    for _, spread in gather:
        spread.step2()
    for k in range(1, shards):
        gather[k - 1][1].finish()
        forward(place.across(k))

    mixn = mixt[...].T
    total = x[...].astype(F32)
    for g in range(shards):
        total = total + nn(mixn[:, g * width : (g + 1) * width], weight(g, 3))
    dres[...] = total

    gain_sum[...] = jnp.zeros_like(gain_sum)

    @pl.loop(0, ROWS // 64)
    def _(i):
        at = pl.ds(pl.multiple_of(i * 64, 64), 64)
        zz, _ = norm_stats(dres[at, :])
        nffn[at, :] = (zz * gain_f[...]).astype(BF)

    BLK = 256

    @pl.loop(0, ROWS // BLK)
    def _(i):
        at = pl.ds(pl.multiple_of(i * BLK, BLK), BLK)
        u = nn(nffn[at, :], wu[...])
        c = cot[at, :]
        dh = nt(c, wd[...])
        cdf = 0.5 + 0.5 * lax.erf(u * SQH)
        h = (u * cdf).astype(BF)
        hidden[at, :] = h
        dinner[at, :] = (dh * (cdf + u * (PHI * jnp.exp(-0.5 * u * u)))).astype(BF)
        out[at, :] = (dres[at, :] + nn(h, wd[...])).astype(BF)

    g_ud[1] = tn(hidden[...], cot[...]).astype(BF)
    g_ud[0] = tn(nffn[...], dinner[...]).astype(BF)
    ud = Halve(link, place, g_ud, r0u, r1u, r2u, rxu)
    ud.start()

    @pl.loop(0, ROWS // BLK)
    def _(i):
        at = pl.ds(pl.multiple_of(i * BLK, BLK), BLK)
        dn = nt(dinner[at, :], wu[...])
        zz, r = norm_stats(dres[at, :])
        gain_sum[1:2, :] += jnp.sum(dn * zz, axis=0, keepdims=True)
        dr = cot[at, :].astype(F32) + norm_back(dn, zz, r, gain_f[...])
        dres[at, :] = dr
        dbr[at, :] = dr.astype(BF)

    dkt[...] = jnp.zeros_like(dkt)
    dvt[...] = jnp.zeros_like(dvt)

    def back(g, s):
        attend_back(
            g, s, slot_meta(mol, fill, z, s), mask, qt, kt, vn, dmt, probs, mixf, dqkv, dkt, dvt, scale
        )

    def halo_copy(side, g):
        return pltpu.make_async_remote_copy(
            src_ref=halo_out.at[side, g], dst_ref=halo_in.at[side, g],
            send_sem=halo_send.at[side, g], recv_sem=halo_recv.at[side, g],
            device_id=after if side else before, device_id_type=MESH,
        )

    def border(g):
        dmt[g] = nt(wg[g, 3 * width : 4 * width, :], dbr[...]).astype(BF)
        back(g, 0)
        back(g, SLOTS_DEV - 1)
        for side, cols in ((0, slice(0, SLOT)), (1, slice(SLOT + ROWS, WIN))):
            halo_out[side, g, 0] = dkt[g, :, cols].astype(BF)
            halo_out[side, g, 1] = dvt[g, :, cols].astype(BF)

        @pl.when(z > 0)
        def _():
            halo_copy(0, g).start()

        @pl.when(z < last)
        def _():
            halo_copy(1, g).start()

    ud_steps = [ud.step1, ud.step2, ud.step3]
    for k in range(shards):
        border(place.across((k + 1) % shards))
        if k < 3:
            ud_steps[k]()

    def quarter(ref, q):
        lane = q % 2
        c0, ca, cb = place.index(0)
        rows = piece_rows(c0, ca + lane * (cb - ca), cb + lane * (ca - cb), lane)
        return ref.at[q // 2, rows]

    z_copies = [
        link.send(quarter(g_ud, place.across(k)), zud.at[k - 1], column(k)) for k in range(1, shards)
    ]
    spread_ud = Spread(link, place, f_ud)
    own_spread = Spread(link, place, f_own)

    def ud_sum():
        for copy in z_copies:
            copy.wait_recv()
        mine = quarter(g_ud, z)
        add_rows(mine, *[zud.at[k] for k in range(shards - 1)])
        quarter(f_ud, z)[...] = mine[...]
        return [link.send(quarter(f_ud, z), quarter(f_ud, z), column(k)) for k in range(1, shards)]

    def ud_spread():
        for copy in z_back:
            copy.wait_recv()
        spread_ud.start()

    def shard_grads(k):
        g = place.across(k)

        @pl.loop(1, SLOTS_DEV - 1)
        def _(s):
            back(g, s)

        @pl.when(z < last)
        def _():
            halo_copy(0, g).wait_recv()
            cols = slice(ROWS, SLOT + ROWS)
            dkt[g, :, cols] += halo_in[0, g, 0].astype(F32)
            dvt[g, :, cols] += halo_in[0, g, 1].astype(F32)

        @pl.when(z > 0)
        def _():
            halo_copy(1, g).wait_recv()
            cols = slice(SLOT, 2 * SLOT)
            dkt[g, :, cols] += halo_in[1, g, 0].astype(F32)
            dvt[g, :, cols] += halo_in[1, g, 1].astype(F32)

        dqkv[g, 1] = dkt[g, :, SLOT : SLOT + ROWS].astype(BF)
        dqkv[g, 2] = dvt[g, :, SLOT : SLOT + ROWS].astype(BF)
        own = nw[SLOT : SLOT + ROWS, :]
        for c in range(3):
            g_k[k, c * width : (c + 1) * width, :] = nn(dqkv[g, c], own).astype(BF)
        at = pl.ds(pl.multiple_of(g * width, 16), width)
        g_k[k, 3 * width : 4 * width, :] = nn(mixt[at, :], dbr[...]).astype(BF)
        job = Halve(link, place, g_k.at[k], r0.at[k], r1.at[k], r2.at[k], rx.at[k])
        job.start()
        return job

    def send_shard(k, job):
        return [link.send(job.mine(lane), zk.at[k - 1, lane], column(k)) for lane in range(2)]

    job1 = shard_grads(1)
    z_back = ud_sum()
    job2 = shard_grads(2)
    job1.step1()
    ud_spread()
    job3 = shard_grads(3)
    job1.step2()
    job2.step1()
    spread_ud.step1()
    job0 = shard_grads(0)
    job1.step3()
    z1 = send_shard(1, job1)
    job2.step2()
    job3.step1()
    spread_ud.step2()

    total = None
    for g in range(shards):
        term = tn(dqkv[g].reshape(3 * width, ROWS), wg[g, : 3 * width, :])
        total = term if total is None else total + term
    dtok[...] = total
    job0.step1()
    job2.step3()
    z2 = send_shard(2, job2)
    job3.step2()

    @pl.loop(0, ROWS // 64)
    def _(i):
        at = pl.ds(pl.multiple_of(i * 64, 64), 64)
        dn = dtok[at, :]
        zz, r = norm_stats(x[at, :].astype(F32))
        gain_sum[0:1, :] += jnp.sum(dn * zz, axis=0, keepdims=True)
        dtok[at, :] = dres[at, :] + norm_back(dn, zz, r, gain_a[...])

    job0.step2()
    job3.step3()
    z3 = send_shard(3, job3)
    spread_ud.finish()

    for bit in range(len(place.bits)):
        copy = link.send(gain_sum, gain_got.at[bit], place.near(bit))
        copy.wait_recv()
        link.done(copy)
        gain_sum[...] += gain_got[bit]
    gain_col[z] = gain_sum[...]
    gain_copies = [link.send(gain_sum, gain_col.at[z], column(k)) for k in range(1, shards)]

    job0.step3()
    for copy in z1 + z2 + z3:
        copy.wait_recv()
    for lane in range(2):
        mine = job0.mine(lane)
        add_rows(mine, *[zk.at[k, lane] for k in range(shards - 1)])
        f_own.at[piece_rows(*place.index(lane), lane)][...] = mine[...]
    own_spread.start()
    own_spread.step1()
    own_spread.step2()
    for copy in gain_copies:
        copy.wait_recv()
    gains_out[...] = sum(gain_col[k] for k in range(shards))
    own_spread.finish()

    link.drain()

    @pl.when(z < last)
    def _():
        to_next.wait_send()
        for g in range(shards):
            halo_copy(1, g).wait_send()

    @pl.when(z > 0)
    def _():
        to_prev.wait_send()
        for g in range(shards):
            halo_copy(0, g).wait_send()


VM = pl.BlockSpec(memory_space=pltpu.VMEM)
SM = pl.BlockSpec(memory_space=pltpu.SMEM)
COPIES = 96


def S(shape, dtype):
    return jax.ShapeDtypeStruct(shape, dtype)


def layer(dp_size, n, width, *operands):
    pairs = width // (2 * HEAD_DIM)
    extra = 1
    step = 8
    more = 0
    while step < dp_size:
        step *= 2
        more += 1
    extra = max(more, 1)
    bits = 3 + more
    V = pltpu.VMEM
    return pl.pallas_call(
        functools.partial(kernel, dp_size, n),
        out_shape=(S((ROWS, D), BF), S((ROWS, D), F32), S((8, D), F32), S((2, D, D), BF), S((D, D), BF)),
        in_specs=[SM, SM] + [VM] * 4 + [pl.BlockSpec(memory_space=pl.ANY)] + [VM] * 2,
        out_specs=(VM,) * 5,
        scratch_shapes=[
            V((n, D, D), BF),
            V((WIN, D), BF),
            V((2, SLOT, D), BF),
            V((pairs, width, 2 * SLOT), BF),
            V((n, width, ROWS), BF),
            V((n, width, WIN), BF),
            V((n, width, WIN), BF),
            V((n, WIN, width), BF),
            V((n, WIN, width), BF),
            V((n, SLOTS_DEV, pairs, 2 * SLOT, 2 * SLOT), BF),
            V((n, width, ROWS), F32),
            V((D, ROWS), BF),
            V((n, width, ROWS), BF),
            V((ROWS, D), BF),
            V((ROWS, D), F32),
            V((n, 3, width, ROWS), BF),
            V((n, width, WIN), F32),
            V((n, width, WIN), F32),
            V((2, n, 2, width, SLOT), BF),
            V((2, n, 2, width, SLOT), BF),
            V((2, D, D), BF),
            V((n, D, D), BF),
            V((2, D // 2, D), BF),
            V((2, 2, 2, LANE, D), BF),
            V((2, 2, LANE, D), BF),
            V((extra, 2, 2, LANE, D), BF),
            V((n, D // 2, D), BF),
            V((n, 2, 2, LANE, D), BF),
            V((n, 2, LANE, D), BF),
            V((n, extra, 2, LANE, D), BF),
            V((n - 1, LANE, D), BF),
            V((n - 1, 2, LANE, D), BF),
            V((8, D), F32),
            V((bits, 8, D), F32),
            V((n, 8, D), F32),
            pltpu.SemaphoreType.DMA((COPIES + 12 * more,)),
            pltpu.SemaphoreType.DMA((COPIES + 12 * more,)),
            pltpu.SemaphoreType.DMA((2, n)),
            pltpu.SemaphoreType.DMA((2, n)),
            pltpu.SemaphoreType.DMA,
        ],
        compiler_params=pltpu.CompilerParams(
            vmem_limit_bytes=67043328, collective_id=0, has_side_effects=True
        ),
        name="layer",
    )(*operands)


def local(tokens_in, gain_attn, gain_ffn, w_qkv, w_out, w_up, w_down, slot_mol, slot_fill, cotangent):
    n = lax.axis_size("head")
    width = w_out.shape[0]
    wown = jnp.concatenate([w_qkv.transpose(0, 2, 1).reshape(3 * width, D), w_out], axis=0)
    out, dtok, gains, ud, own = layer(
        lax.axis_size("dp"), n, width,
        slot_mol, slot_fill, tokens_in, cotangent, gain_attn[None], gain_ffn[None], wown, w_up, w_down,
    )
    own = own.astype(F32)
    ud = ud.astype(F32)
    gqkv = own[: 3 * width].reshape(3, width, D).transpose(0, 2, 1)
    return (out, dtok, gains[0], gains[1], gqkv, own[3 * width :], ud[0], ud[1])


def solution(mesh):
    return jax.shard_map(
        local,
        mesh=mesh,
        in_specs=(
            P(("dp", "head"), None), P(), P(), P(None, None, "head"), P("head", None), P(), P(),
            P("dp", None), P("dp", None), P(("dp", "head"), None),
        ),
        out_specs=(
            P(("dp", "head"), None), P(("dp", "head"), None), P(), P(), P(None, None, "head"), P("head", None), P(), P(),
        ),
        check_vma=False,
    )
```

time: 746 us -> 160 us (0.21)
  waiting for transfers between devices: 449 us -> 0 us
  Pallas kernels: 0 us -> 145 us
  matrix products: 143 us -> 0 us
  other arithmetic: 46.8 us -> 4.38 us
  blocking collectives: 40.9 us -> 0 us
  local copies, waits for them, and re-layouts: 37.4 us -> 9.3 us
  between operations: 14.6 us -> 0.68 us
  loops' own time: 13.1 us -> 0 us
    psum x2 -> x0, waiting for transfers between devices: 168 us -> none  [the longest x1 102 us: local(): lax.psum((grad_up, grad_down, grad_gain_attn, grad_gain_ffn), ('dp', 'hea...]
    reduce_scatter x2 -> x0, waiting for transfers between devices: 151 us -> none  [the longest x1 109 us: local(): lax.psum_scatter(jnp.dot(mixed_rows, w_out, preferred_element_type=jnp.fl...]
    pallas_call x0 -> x1, Pallas kernels: none -> 145 us  [layer(): pl.pallas_call(functools.partial(kernel, dp_size, n), out_shape=(S((ROWS,...]
    dot_general x39 -> x0, matrix products: 139 us -> none  [the longest x8 23.2 us: scores_of(): jnp.einsum('qhe,khe->hqk', query_block, key_block, preferred_element_type...]
    all_gather x2 -> x0, waiting for transfers between devices: 130 us -> none  [the longest x1 66.1 us: local(): gathered = lax.all_gather(normed_low, 'head', axis=0, tiled=True)]
    psum x1 -> x0, blocking collectives: 40.9 us -> none  [local(): lax.psum((grad_up, grad_down, grad_gain_attn, grad_gain_ffn), ('dp', 'hea...]
    reduce_sum x11 -> x0, other arithmetic: 21.9 us -> none  [the longest x4 12 us: attend(): row_sum = jnp.sum(exp_scores, axis=-1, keepdims=True)]
    convert_element_type x8 -> x1, other arithmetic: 17.4 us -> 2.02 us  [local(): ud = ud.astype(F32)]
  transfers between devices with their start and end apart: 6 -> 0, of which waited for: 6 -> 0; matrix products, arithmetic and copies ran while one was open for 3% -> 0% of each run, Pallas kernels for 0% -> 0%
where the time goes in v1:
time: 160 us; the launch traced here: 159 us
  Pallas kernels  145 us (91%)
  local copies, waits for them, and re-layouts  9.3 us (6%)
  other arithmetic  4.38 us (3%)
    pallas_call x1, Pallas kernels, layer(): pl.pallas_call(functools.partial(kernel, dp_size, n), out_shape=(S((ROWS,...  145 us

profile of v1, /device:TPU:0, one launch (start us, length us, event | category | flops | bytes accessed | tf_op | source)
XLA Modules:
  0.0 159.3 jit_solution(17202740592375681205)
XLA Ops:
  0.6 0.0 copy-start.3
  0.6 0.0 copy-start.4
  0.7 2.4 %pad_maximum_fusion.wown = bf16[768,768]{1,0:T(8,128)(2,1)} fusion(bf16[192,768]{1,0:T(8,128)(2,1)} %param.14, bf16[576,768]{1,0:T(8,128)(2,1)} %bitcast.11), kind=kLoop, calls=%fused_computation.2 | loop fusion | flops 2359296 | bytes 2359296 | tf_op jit(solution)/shard_map/concatenate | solution.py:745
  3.0 0.0 copy-done.3
  3.0 0.6 broadcast_in_dim.6.gain_a
  3.6 0.0 copy-done.4
  3.6 0.6 broadcast_in_dim.7.gain_f
  4.2 144.9 %layer.1 = (bf16[512,768]{1,0:T(8,128)(2,1)}, f32[512,768]{1,0:T(8,128)}, f32[8,768]{1,0:T(8,128)}, bf16[2,768,768]{2,1,0:T(8,128)(2,1)}, bf16[768,768]{1,0:T(8,128)(2,1)}) custom-call(s32[1,16]{1,0:T(1,128)} %mol.1, s32[1,16]{1,0:T(1,128)} %fill.1, bf16[512,768]{1,0:T(8,128)(2,1)} %x.1, bf16[512,768]{1,0:T(8,128)(2,1)} %cot.1, ...), custom_call_target="tpu_custom_call" | custom-call | tf_op jit(solution)/shard_map/layer/pallas_call | solution.py:688
  149.1 2.0 %convert_element_type.7 = f32[2,768,768]{2,1,0:T(8,128)S(1)} convert(bf16[2,768,768]{2,1,0:T(8,128)(2,1)} %get-tuple-element.17) | non-fusion elementwise | flops 1179648 | bytes 7077888 | tf_op jit(solution)/shard_map/convert_element_type | solution.py:751
  151.1 0.0 copy-start
  151.1 2.5 %slice_bitcast_fusion = (f32[768,768]{1,0:T(8,128)}, f32[768,768]{1,0:T(8,128)}) fusion(f32[2,768,768]{2,1,0:T(8,128)S(1)} %convert_element_type.7), kind=kLoop, calls=%fused_computation | loop fusion | bytes 9437184 | tf_op jit(solution)/shard_map/squeeze | solution.py:753
  153.6 0.0 copy-done
  153.6 0.0 copy-start.2
  153.6 0.0 copy-start.1
  153.6 1.3 slice.24
  155.0 0.9 slice.25
  155.8 1.4 slice_reduce_fusion
  157.3 0.0 copy-done.2
  157.3 0.9 copy.20
  158.1 0.0 copy-done.1
  158.1 1.1 copy.21
Async XLA Ops:
  0.6 2.4 %copy-start.3 = (f32[768]{0:T(1024)S(1)}, f32[768]{0:T(1024)}, u32[]{:S(2)}) copy-start(f32[768]{0:T(1024)} %param.11) | copy-start | bytes 9220
  0.6 3.0 %copy-start.4 = (f32[768]{0:T(1024)S(1)}, f32[768]{0:T(1024)}, u32[]{:S(2)}) copy-start(f32[768]{0:T(1024)} %param.12) | copy-start | bytes 9220
  151.1 2.5 %copy-start = (bf16[768,768]{1,0:T(8,128)(2,1)S(1)}, bf16[768,768]{1,0:T(8,128)(2,1)}, u32[]{:S(2)}) copy-start(bf16[768,768]{1,0:T(8,128)(2,1)} %get-tuple-element.16) | copy-start | bytes 3538948
  153.6 3.6 %copy-start.2 = (bf16[512,768]{1,0:T(8,128)(2,1)S(1)}, bf16[512,768]{1,0:T(8,128)(2,1)}, u32[]{:S(2)}) copy-start(bf16[512,768]{1,0:T(8,128)(2,1)} %get-tuple-element.30) | copy-start | bytes 2359300
  153.6 4.5 %copy-start.1 = (f32[512,768]{1,0:T(8,128)S(1)}, f32[512,768]{1,0:T(8,128)}, u32[]{:S(2)}) copy-start(f32[512,768]{1,0:T(8,128)} %get-tuple-element.31) | copy-start | bytes 4718596

commit v2 on v1

v2 whole, which is shorter than its diff:
```python
import functools

import jax
import jax.numpy as jnp
from jax import lax
from jax.experimental import pallas as pl
from jax.experimental.pallas import tpu as pltpu
from jax.sharding import PartitionSpec as P

HEAD_DIM = 24
SLOT = 128
D = 768
EPS = 1e-05
SLOTS_DEV = 4
ROWS = SLOTS_DEV * SLOT
WIN = ROWS + 2 * SLOT
BF = jnp.bfloat16
F32 = jnp.float32


def nn(a, b):
    return jnp.dot(a, b, preferred_element_type=F32)


def nt(a, b):
    return lax.dot_general(a, b, (((1,), (1,)), ((), ())), preferred_element_type=F32)


def tn(a, b):
    return lax.dot_general(a, b, (((0,), (0,)), ((), ())), preferred_element_type=F32)


def norm_stats(v):
    mean = jnp.mean(v, axis=-1, keepdims=True)
    centred = v - mean
    var = jnp.mean(centred * centred, axis=-1, keepdims=True)
    r = lax.rsqrt(var + EPS)
    return centred * r, r


def norm_back(grad, z, r, gain):
    e = grad * gain
    return r * (e - jnp.mean(e, -1, keepdims=True) - z * jnp.mean(e * z, -1, keepdims=True))


WIDER = 64


def build_masks(mask_ref, width):
    shape = mask_ref.shape[1:]
    rows = lax.broadcasted_iota(jnp.int32, shape, 0)
    right = (lax.broadcasted_iota(jnp.int32, shape, 1) >= SLOT).astype(jnp.int32)
    for p in range(mask_ref.shape[0]):
        low = (2 * p + right) * HEAD_DIM
        keep = ((rows >= low) & (rows < low + HEAD_DIM)) | (rows >= width)
        mask_ref[p] = jnp.where(keep, 1.0, 0.0).astype(BF)


def extend(fill_ref, z, width, qt, kt, vt, kn, vn):
    lane = lax.broadcasted_iota(jnp.int32, (SLOT, WIDER), 1)
    row = lax.broadcasted_iota(jnp.int32, (SLOT, WIDER), 0)
    ones = jnp.where(lane < 2, 1.0, 0.0).astype(BF)
    top = lax.broadcasted_iota(jnp.int32, (WIDER, ROWS), 0)
    first = jnp.where(top == 0, 1.0, 0.0).astype(BF)
    slots = (WIN + SLOT) // SLOT
    for g in range(qt.shape[0]):
        qt[g, width:, :] = first
        kn[g, WIN:, :width] = jnp.zeros((SLOT, width), BF)
    for s in range(slots):
        live = 0
        if s < slots - 1:
            at = jnp.minimum(jnp.maximum(z * SLOTS_DEV + s - 1, 0), fill_ref.shape[1] - 1)
            live = fill_ref[0, at]
        bias = jnp.where((lane == 0) & (row >= live), -1e30, 0.0).astype(BF)
        for g in range(qt.shape[0]):
            kn[g, s * SLOT : (s + 1) * SLOT, width:] = bias
            if s < slots - 1:
                vn[g, s * SLOT : (s + 1) * SLOT, width:] = ones


def slot_meta(mol_ref, z, s):
    at = z * SLOTS_DEV + s
    last = mol_ref.shape[1] - 1
    before, after = jnp.maximum(at - 1, 0), jnp.minimum(at + 1, last)
    mine = mol_ref[0, at]
    prev = jnp.where((mol_ref[0, before] == mine) & (at > 0), 1, 0)
    nxt = jnp.where((mol_ref[0, after] == mine) & (at < last), 1, 0)
    return prev, nxt * (1 - prev)


def chosen(*terms):
    total = None
    for flag, block in terms:
        term = jnp.broadcast_to(flag.astype(F32), block.shape).astype(BF) * block
        total = term if total is None else total + term
    return total


def pair_rows(full):
    rows = lax.broadcasted_iota(jnp.int32, (2 * HEAD_DIM, SLOT), 0)
    return jnp.where(rows < HEAD_DIM, full[:, :SLOT], full[:, SLOT:])


def project(g, parts, nw, low, count, qt, kt, vt, kn, vn, scale):
    width = kt.shape[1]
    at = slice(low, low + count)
    if parts[0] is not None:
        qt[g, :width, :] = (nt(parts[0], nw[pl.ds(SLOT, ROWS), :]) * scale).astype(BF)
    for part, wide, tall in ((parts[1], kt, kn), (parts[2], vt, vn)):
        rows = nt(part, nw[at, :]).astype(BF)
        wide[g, :, at] = rows
        tall[g, at, :width] = rows.T


def windows(s):
    own = pl.multiple_of((s + 1) * SLOT, SLOT)
    before = pl.multiple_of(s * SLOT, SLOT)
    after = pl.multiple_of((s + 2) * SLOT, SLOT)
    return pl.ds(own, SLOT), pl.ds(before, SLOT), pl.ds(after, SLOT), pl.ds(before, SLOT)


def attend(g, s, meta, mask, qt, kn, vt, probs, share, mixf, mixt):
    prev, nxt = meta
    own, before, after, mine = windows(s)
    width = vt.shape[1]
    partner = chosen((prev, kn[g, before, :]), (nxt, kn[g, after, :]), (1 - prev - nxt, kn[g, WIN:, :]))
    keys = jnp.concatenate([kn[g, own, :], partner], axis=0)
    vals = jnp.concatenate([vt[g, :, own], chosen((prev, vt[g, :, before]), (nxt, vt[g, :, after]))], axis=1)
    ones = jnp.ones((16, 2 * SLOT), BF)
    q = qt[g, :, mine]
    q2 = jnp.concatenate([q, q], axis=1)
    for p in range(mask.shape[0]):
        scores = nn(keys, q2 * mask[p])
        top = jnp.max(scores, axis=0, keepdims=True)
        ex = jnp.exp(scores - top).astype(BF)
        probs[g, s, p] = ex
        head_rows = slice(2 * HEAD_DIM * p, 2 * HEAD_DIM * (p + 1))
        both = nn(jnp.concatenate([vals[head_rows, :], ones], axis=0), ex)
        part = pair_rows(jnp.broadcast_to(1.0 / both[2 * HEAD_DIM : 2 * HEAD_DIM + 1, :], (2 * HEAD_DIM, 2 * SLOT)))
        mixed = pair_rows(both[: 2 * HEAD_DIM, :]) * part
        share[g, head_rows, mine] = part
        mixf[g, head_rows, mine] = mixed
        at = pl.ds(pl.multiple_of(g * width + 2 * HEAD_DIM * p, 16), 2 * HEAD_DIM)
        mixt[at, mine] = mixed.astype(BF)


def attend_back(g, s, meta, mask, qt, kt, vn, dmt, probs, share, mixf, dqkv, dkt, dvt, scale):
    prev, nxt = meta
    own, before, after, mine = windows(s)
    width = dmt.shape[1]
    fprev, fnext = prev.astype(F32), nxt.astype(F32)
    vals = jnp.concatenate([vn[g, own, :], chosen((prev, vn[g, before, :]), (nxt, vn[g, after, :]))], axis=0)
    keys = jnp.concatenate([kt[g, :, own], chosen((prev, kt[g, :, before]), (nxt, kt[g, :, after]))], axis=1)
    q = qt[g, :width, mine]
    dm = (dmt[g, :, mine].astype(F32) * share[g, :, mine]).astype(BF)
    q2 = jnp.concatenate([q, q], axis=1)
    dm2 = jnp.concatenate([dm, dm], axis=1)
    prod = dm.astype(F32) * mixf[g, :, mine]
    line = lax.broadcasted_iota(jnp.int32, (16, 2 * SLOT), 0)
    rest = jnp.zeros((WIDER - 16, 2 * SLOT), BF)
    for p in range(mask.shape[0]):
        head_rows = slice(2 * HEAD_DIM * p, 2 * HEAD_DIM * (p + 1))
        mid = 2 * HEAD_DIM * p + HEAD_DIM
        inner = jnp.concatenate(
            [
                jnp.sum(prod[2 * HEAD_DIM * p : mid], axis=0, keepdims=True),
                jnp.sum(prod[mid : mid + HEAD_DIM], axis=0, keepdims=True),
            ],
            axis=1,
        )
        high = inner.astype(BF).astype(F32)
        take_off = jnp.where(line == 0, -high, jnp.where(line == 1, high - inner, 0.0)).astype(BF)
        rhs = dm2 * mask[p, :width, :]
        d_probs = nn(vals, jnp.concatenate([rhs, take_off, rest], axis=0))
        pr = probs[g, s, p]
        d_scores = pr * d_probs.astype(BF)
        dq = pair_rows(nn(keys[head_rows, :], d_scores)) * scale
        dqkv[g, 0, head_rows, mine] = dq.astype(BF)
        qm = (q2 * mask[p, :width, :])[head_rows, :]
        dk = nt(qm, d_scores)
        dv = nt(rhs[head_rows, :], pr)
        dkt[g, head_rows, own] += dk[:, :SLOT]
        dvt[g, head_rows, own] += dv[:, :SLOT]
        dkt[g, head_rows, before] += fprev * dk[:, SLOT:]
        dvt[g, head_rows, before] += fprev * dv[:, SLOT:]
        dkt[g, head_rows, after] += fnext * dk[:, SLOT:]
        dvt[g, head_rows, after] += fnext * dv[:, SLOT:]


SQH = 0.7071067811865476
PHI = 0.3989422804014327
MESH = pl.DeviceIdType.MESH
HALVINGS = 3
PIECE = D // 8
LANE = PIECE // 2


class Link:
    def __init__(self, send_sem, recv_sem):
        self.send_sem, self.recv_sem, self.used, self.open = send_sem, recv_sem, 0, []

    def reserve(self, count):
        self.used += count
        return self.used - count

    def make(self, src, dst, target, slot=None):
        slot = self.reserve(1) if slot is None else slot
        return pltpu.make_async_remote_copy(
            src_ref=src, dst_ref=dst, send_sem=self.send_sem.at[slot], recv_sem=self.recv_sem.at[slot],
            device_id=target, device_id_type=MESH,
        )

    def send(self, src, dst, target):
        copy = self.make(src, dst, target)
        copy.start()
        self.open.append(copy)
        return copy

    def done(self, copy):
        copy.wait_send()
        self.open = [c for c in self.open if c is not copy]

    def drain(self):
        for copy in self.open:
            copy.wait_send()
        self.open = []


def add_rows(dst, *terms):
    @pl.loop(0, dst.shape[0] // 16)
    def _(i):
        at = pl.ds(pl.multiple_of(i * 16, 16), 16)
        total = dst[at, :].astype(F32)
        for term in terms:
            total = total + term[at, :].astype(F32)
        dst[at, :] = total.astype(dst.dtype)


def piece_rows(d0, d1, d2, lane):
    return pl.ds(pl.multiple_of(((d0 * 2 + d1) * 2 + d2) * PIECE + lane * LANE, 16), LANE)


class Place:
    def __init__(self, dp_size, shards):
        self.dp = lax.axis_index("dp")
        self.z = lax.axis_index("head")
        self.shards = shards
        self.bits, self.partner = [], []
        step = 1
        while step < dp_size:
            bit = (self.dp // step) % 2
            self.bits.append(bit)
            self.partner.append(self.dp + step - 2 * step * bit)
            step *= 2
        self.order = ((0, 1, 2), (0, 2, 1))

    def near(self, bit):
        return {"dp": self.partner[bit]}

    def across(self, k):
        step, found = 1, 0
        while step < self.shards:
            found = found + step * ((self.z // step + k // step) % 2)
            step *= 2
        return found

    def index(self, lane):
        return tuple(self.bits[b] for b in self.order[lane])


class Halve:
    def __init__(self, link, place, g, r0, r1, r2, rx):
        self.link, self.place, self.g, self.r0, self.r1, self.r2, self.rx = link, place, g, r0, r1, r2, rx

    def start(self):
        p = self.place
        self.pass_on, self.keep = [], []
        for side, out in ((1, self.pass_on), (0, self.keep)):
            for lane in range(2):
                c0, c1, _ = p.index(lane)
                d1 = c1 + side * (1 - 2 * c1)
                out.append(
                    [
                        self.link.send(
                            self.g.at[piece_rows(1 - c0, d1, b, lane)], self.r0.at[piece_rows(0, d1, b, lane)], p.near(0)
                        )
                        for b in range(2)
                    ]
                )

    def mine(self, lane):
        return self.g.at[piece_rows(*self.place.index(lane), lane)]

    def step1(self):
        p = self.place
        self.copies = []
        for lane in range(2):
            c0, c1, _ = p.index(lane)
            sent = []
            for b in range(2):
                self.pass_on[lane][b].wait_recv()
                part = self.g.at[piece_rows(c0, 1 - c1, b, lane)]
                add_rows(part, self.r0.at[piece_rows(0, 1 - c1, b, lane)])
                sent.append(self.link.send(part, self.r1.at[lane, b], p.near(p.order[lane][1])))
            self.copies.append(sent)

    def step2(self, finish=None, r_last=None):
        p = self.place
        old, self.copies = self.copies, []
        for lane in range(2):
            c0, c1, c2 = p.index(lane)
            for b in range(2):
                self.keep[lane][b].wait_recv()
                old[lane][b].wait_recv()
            if finish is not None:
                for b in range(2):
                    part = self.g.at[piece_rows(c0, c1, b, lane)]
                    add_rows(part, self.r0.at[piece_rows(0, c1, b, lane)], self.r1.at[lane, b])
                finish(lane)
                self.copies.append(
                    [
                        self.link.send(self.g.at[piece_rows(c0, c1, b, lane)], r_last.at[lane, b], p.near(p.order[lane][2]))
                        for b in range(2)
                    ]
                )
                continue
            part = self.g.at[piece_rows(c0, c1, 1 - c2, lane)]
            add_rows(part, self.r0.at[piece_rows(0, c1, 1 - c2, lane)], self.r1.at[lane, 1 - c2])
            self.copies.append(self.link.send(part, self.r2.at[lane], p.near(p.order[lane][2])))

    def step3(self):
        p = self.place
        for lane in range(2):
            _, c1, c2 = p.index(lane)
            self.copies[lane].wait_recv()
            add_rows(self.mine(lane), self.r0.at[piece_rows(0, c1, c2, lane)], self.r1.at[lane, c2], self.r2.at[lane])
        for extra in range(HALVINGS, len(p.bits)):
            copies = [
                self.link.send(self.mine(lane), self.rx.at[extra - HALVINGS, lane], p.near(extra)) for lane in range(2)
            ]
            for lane in range(2):
                copies[lane].wait_recv()
                self.link.done(copies[lane])
                add_rows(self.mine(lane), self.rx.at[extra - HALVINGS, lane])


    def step3_both(self, r_last, spread):
        p = self.place
        spread.begin()
        for lane in range(2):
            c0, c1, c2 = p.index(lane)
            for b in range(2):
                self.copies[lane][b].wait_recv()
            for b in range(2):
                rows = piece_rows(c0, c1, b, lane)
                self.link.done(self.copies[lane][b])
                add_rows(self.g.at[rows], r_last.at[lane, b])
                spread.f.at[rows][...] = self.g.at[rows][...]
            for b in range(2):
                spread.pass_on(lane, piece_rows(c0, c1, b, lane))


class Spread:
    def __init__(self, link, place, f):
        self.link, self.place, self.f = link, place, f

    def swap(self, rows, bit):
        part = self.f.at[rows]
        return self.link.send(part, part, self.place.near(bit))

    def begin(self):
        self.first, self.second, self.core = [], [[], []], []

    def pass_on(self, lane, rows):
        self.second[lane].append(self.swap(rows, self.place.order[lane][1]))
        self.core.append(self.swap(rows, 0))

    def start(self):
        p = self.place
        self.begin()
        for lane in range(2):
            own = piece_rows(*p.index(lane), lane)
            self.first.append(self.swap(own, p.order[lane][2]))
            self.pass_on(lane, own)

    def step1(self):
        p = self.place
        for lane in range(2):
            c0, c1, c2 = p.index(lane)
            self.first[lane].wait_recv()
            self.pass_on(lane, piece_rows(c0, c1, 1 - c2, lane))

    def step2(self):
        p = self.place
        for lane in range(2):
            c0, c1, c2 = p.index(lane)
            for copy in self.second[lane]:
                copy.wait_recv()
            for b in range(2):
                self.core.append(self.swap(piece_rows(c0, 1 - c1, b, lane), 0))

    def finish(self):
        for copy in self.core:
            copy.wait_recv()


def kernel(
    dp_size, shards,
    mol, fill, x, cot_in, gain_a, gain_f, qkv_in, wo_in, wu_in, wd_in,
    out_to, dtok_to, gains_out, up_to, down_to, own_to,
    wg, cot, wu, wd, f_ud, f_own,
    nw, xh, mask, qt, kt, vt, kn, vn, probs, share, mixf, mixt, dmt, dbr, dres,
    dqkv, dkt, dvt, halo_out, halo_in, g_ud, g_k, r0, r1, r2, rx, r_last, zud, zk,
    gain_sum, gain_got, gain_col,
    send_sem, recv_sem, halo_send, halo_recv, load_sem,
):
    place = Place(dp_size, shards)
    link = Link(send_sem, recv_sem)
    z = place.z
    last = shards - 1
    nffn, hidden, dinner, out = (g_k.at[i, pl.ds(0, ROWS)] for i in range(4))
    scale = HEAD_DIM ** (-0.5)
    width = dmt.shape[1]

    def column(k):
        return {"head": place.across(k)}

    moves = []

    def move(src, dst):
        copy = pltpu.make_async_copy(src, dst, load_sem.at[len(moves)])
        copy.start()
        moves.append(copy)
        return copy

    own_w = [
        move(qkv_in, wg.at[z, pl.ds(0, 3 * width)]),
        move(wo_in, wg.at[z, pl.ds(3 * width, width)]),
    ]
    ffn_w = [move(wu_in, wu), move(wd_in, wd), move(cot_in, cot)]

    barrier = pltpu.get_barrier_semaphore()
    peers = [place.near(b) for b in range(len(place.bits))] + [column(k) for k in range(1, shards)]
    for peer in peers:
        pl.semaphore_signal(barrier, inc=1, device_id=peer, device_id_type=MESH)
    pl.semaphore_wait(barrier, len(peers))

    after = {"head": jnp.minimum(z + 1, last)}
    before = {"head": jnp.maximum(z - 1, 0)}
    to_next = link.make(x.at[pl.ds(ROWS - SLOT, SLOT)], xh.at[0], after)
    to_prev = link.make(x.at[pl.ds(0, SLOT)], xh.at[1], before)

    for copy in own_w:
        copy.wait()
    lanes = [piece_rows(*place.index(lane), lane) for lane in range(2)]
    inner = (z > 0) & (z < last)
    outer = (z == 0) | (z == last)
    near_z = [place.across(1), 2 - z // 2, last - last * (z // 2)]
    line = link.reserve(max(10, 2 * shards))
    passed = []

    def along(g, target, step):
        return [
            pltpu.make_async_remote_copy(
                src_ref=wg.at[g, rows], dst_ref=wg.at[g, rows],
                send_sem=send_sem.at[line + 2 * step + lane], recv_sem=recv_sem.at[line + 2 * g + lane],
                device_id={"head": target}, device_id_type=MESH,
            )
            for lane, rows in enumerate(lanes)
        ]

    def pass_on(keep, g, target, step):
        copies = along(g, target, step)
        passed.append((keep, copies))

        @pl.when(keep)
        def _():
            for copy in copies:
                copy.start()

    def arrived(g):
        for copy in along(g, after["head"], 0):
            copy.wait_recv()

    pass_on(z < last, z, after["head"], 0)
    pass_on(z > 0, z, before["head"], 1)
    spread = [None] + [Spread(link, place, wg.at[g]) for g in near_z]

    def pick_up(step):
        first, second, third = near_z
        if step == 1:
            arrived(first)
            pass_on(inner, first, last - z, 2)

            @pl.when(inner)
            def _():
                arrived(second)

            pass_on(inner, second, last * (z // 2), 3)
        if step == 2:

            @pl.when(outer)
            def _():
                arrived(second)

            @pl.when(inner)
            def _():
                arrived(third)

            pass_on(inner, third, last * (z // 2), 4)
        if step == 3:

            @pl.when(outer)
            def _():
                arrived(third)

        spread[step].start()

    build_masks(mask, width)
    extend(fill, z, width, qt, kt, vt, kn, vn)

    def normed(at_w, ref, at):
        zz, _ = norm_stats(ref[at, :].astype(F32))
        nw[at_w, :] = (zz * gain_a[...].reshape(1, D)).astype(BF)

    @pl.loop(0, ROWS // 64)
    def _(i):
        at = pl.multiple_of(i * 64, 64)
        normed(pl.ds(at + SLOT, 64), x, pl.ds(at, 64))

    @pl.when(z < last)
    def _():
        to_next.start()

    @pl.when(z > 0)
    def _():
        to_prev.start()

    def weight(g, c):
        return wg[g, c * width : (c + 1) * width, :]

    def heads_mix(g, low, high, step=1):
        @pl.loop(0, (high - low) // step)
        def _(i):
            s = low + i * step
            attend(g, s, slot_meta(mol, z, s), mask, qt, kn, vt, probs, share, mixf, mixt)

    project(z, [weight(z, c) for c in range(3)], nw, SLOT, ROWS, qt, kt, vt, kn, vn, scale)
    heads_mix(z, 1, SLOTS_DEV - 1)
    pick_up(1)

    @pl.when(z > 0)
    def _():
        to_next.wait_recv()

    @pl.when(z == 0)
    def _():
        xh[0] = jnp.zeros_like(xh[0])

    @pl.when(z < last)
    def _():
        to_prev.wait_recv()

    @pl.when(z == last)
    def _():
        xh[1] = jnp.zeros_like(xh[1])

    @pl.loop(0, SLOT // 64)
    def _(i):
        at = pl.multiple_of(i * 64, 64)
        normed(pl.ds(at, 64), xh.at[0], pl.ds(at, 64))
        normed(pl.ds(at + SLOT + ROWS, 64), xh.at[1], pl.ds(at, 64))

    for low in (0, SLOT + ROWS):
        project(z, [None, weight(z, 1), weight(z, 2)], nw, low, SLOT, qt, kt, vt, kn, vn, scale)
    spread[1].step1()
    pick_up(2)
    heads_mix(z, 0, 2 * (SLOTS_DEV - 1), SLOTS_DEV - 1)

    def heads_in(g):
        project(g, [weight(g, c) for c in range(3)], nw, 0, WIN, qt, kt, vt, kn, vn, scale)

    spread[1].step2()
    spread[2].step1()
    pick_up(3)
    spread[1].finish()
    heads_in(near_z[0])
    spread[2].step2()
    spread[3].step1()
    heads_mix(near_z[0], 0, SLOTS_DEV)
    spread[2].finish()
    spread[3].step2()
    heads_in(near_z[1])
    heads_mix(near_z[1], 0, SLOTS_DEV)
    spread[3].finish()
    heads_in(near_z[2])
    heads_mix(near_z[2], 0, SLOTS_DEV)

    mixn = mixt[...].T
    total = x[...].astype(F32)
    for g in range(shards):
        total = total + nn(mixn[:, g * width : (g + 1) * width], weight(g, 3))
    dres[...] = total

    gain_sum[...] = jnp.zeros_like(gain_sum)

    @pl.loop(0, ROWS // 64)
    def _(i):
        at = pl.ds(pl.multiple_of(i * 64, 64), 64)
        zz, _ = norm_stats(dres[at, :])
        nffn[at, :] = (zz * gain_f[...].reshape(1, D)).astype(BF)

    BLK = 256
    for copy in ffn_w:
        copy.wait()

    @pl.loop(0, ROWS // BLK)
    def _(i):
        at = pl.ds(pl.multiple_of(i * BLK, BLK), BLK)
        u = nn(nffn[at, :], wu[...])
        c = cot[at, :]
        dh = nt(c, wd[...])
        cdf = 0.5 + 0.5 * lax.erf(u * SQH)
        h = (u * cdf).astype(BF)
        hidden[at, :] = h
        dinner[at, :] = (dh * (cdf + u * (PHI * jnp.exp(-0.5 * u * u)))).astype(BF)
        out[at, :] = (dres[at, :] + nn(h, wd[...])).astype(BF)

    out_move = move(out, out_to)
    g_ud[1] = tn(hidden[...], cot[...]).astype(BF)
    down = Halve(link, place, g_ud.at[1], *(r.at[shards + 1] for r in (r0, r1, r2, rx)))
    down.start()
    g_ud[0] = tn(nffn[...], dinner[...]).astype(BF)
    up = Halve(link, place, g_ud.at[0], *(r.at[shards] for r in (r0, r1, r2, rx)))
    up.start()
    down.step1()

    @pl.loop(0, ROWS // BLK)
    def _(i):
        at = pl.ds(pl.multiple_of(i * BLK, BLK), BLK)
        dn = nt(dinner[at, :], wu[...])
        zz, r = norm_stats(dres[at, :])
        gain_sum[1:2, :] += jnp.sum(dn * zz, axis=0, keepdims=True)
        dr = cot[at, :].astype(F32) + norm_back(dn, zz, r, gain_f[...].reshape(1, D))
        dres[at, :] = dr
        dbr[at, :] = dr.astype(BF)

    up.step1()
    dkt[...] = jnp.zeros_like(dkt)
    dvt[...] = jnp.zeros_like(dvt)

    def back(g, s):
        attend_back(
            g, s, slot_meta(mol, z, s), mask, qt, kt, vn, dmt, probs, share, mixf, dqkv, dkt, dvt, scale
        )

    def halo_copy(side, g):
        return pltpu.make_async_remote_copy(
            src_ref=halo_out.at[side, g], dst_ref=halo_in.at[side, g],
            send_sem=halo_send.at[side, g], recv_sem=halo_recv.at[side, g],
            device_id=after if side else before, device_id_type=MESH,
        )

    def border(g):
        dmt[g] = nt(wg[g, 3 * width : 4 * width, :], dbr[...]).astype(BF)

        @pl.loop(0, 2)
        def _(i):
            back(g, i * (SLOTS_DEV - 1))

        for side, cols in ((0, slice(0, SLOT)), (1, slice(SLOT + ROWS, WIN))):
            halo_out[side, g, 0] = dkt[g, :, cols].astype(BF)
            halo_out[side, g, 1] = dvt[g, :, cols].astype(BF)

        @pl.when(z > 0)
        def _():
            halo_copy(0, g).start()

        @pl.when(z < last)
        def _():
            halo_copy(1, g).start()

    def middle(g):
        @pl.loop(1, SLOTS_DEV - 1)
        def _(s):
            back(g, s)

    def shard_grads(k, g):
        @pl.when(z < last)
        def _():
            halo_copy(0, g).wait_recv()
            cols = slice(ROWS, SLOT + ROWS)
            dkt[g, :, cols] += halo_in[0, g, 0].astype(F32)
            dvt[g, :, cols] += halo_in[0, g, 1].astype(F32)

        @pl.when(z > 0)
        def _():
            halo_copy(1, g).wait_recv()
            cols = slice(SLOT, 2 * SLOT)
            dkt[g, :, cols] += halo_in[1, g, 0].astype(F32)
            dvt[g, :, cols] += halo_in[1, g, 1].astype(F32)

        dqkv[g, 1] = dkt[g, :, SLOT : SLOT + ROWS].astype(BF)
        dqkv[g, 2] = dvt[g, :, SLOT : SLOT + ROWS].astype(BF)
        own = nw[SLOT : SLOT + ROWS, :]
        for c in range(3):
            g_k[k, c * width : (c + 1) * width, :] = nn(dqkv[g, c], own).astype(BF)
        at = pl.ds(pl.multiple_of(g * width, 16), width)
        g_k[k, 3 * width : 4 * width, :] = nn(mixt[at, :], dbr[...]).astype(BF)
        job = Halve(link, place, *(r.at[k] for r in (g_k, r0, r1, r2, rx)))
        job.start()
        return job

    def quarter(ref, q):
        lane = q % 2
        c0, ca, cb = place.index(0)
        rows = piece_rows(c0, ca + lane * (cb - ca), cb + lane * (ca - cb), lane)
        return ref.at[rows, pl.ds(pl.multiple_of(q // 2 * (D // 2), 128), D // 2)]

    class Column:
        def __init__(self, i):
            self.g, self.got, self.f, self.spread = g_ud.at[i], zud.at[i], f_ud.at[i], Spread(link, place, f_ud.at[i])

        def send(self):
            self.copies = [
                link.send(quarter(self.g, place.across(k)), self.got.at[k - 1], column(k)) for k in range(1, shards)
            ]

        def sum(self):
            for copy in self.copies:
                copy.wait_recv()
            mine, dst = quarter(self.g, z), quarter(self.f, z)
            add_rows(mine, *[self.got.at[k] for k in range(shards - 1)])
            dst[...] = mine[...]
            self.copies = [link.send(dst, dst, column(k)) for k in range(1, shards)]

        def start(self):
            for copy in self.copies:
                copy.wait_recv()
            self.spread.start()

    up_z, down_z = Column(0), Column(1)
    own_spread = Spread(link, place, f_own)

    upper = (z * 2) // shards
    turn = [1 + upper, 2 + upper, 3 - 2 * upper]
    z_slot = link.reserve(2 * (shards - 1))

    def z_copy(k, lane, src):
        return link.make(src, zk.at[k - 1, lane], column(k), z_slot + 2 * (k - 1) + lane)

    def send_shard(i, job):
        for lane in range(2):
            copy = z_copy(turn[i], lane, job.mine(lane))
            copy.start()
            link.open.append(copy)

    g1, g2, g3 = (place.across(k) for k in turn)
    border(0)
    down.step2()
    border(1)
    up.step2()
    middle(g1)
    down.step3()
    down_z.send()
    job1 = shard_grads(1, g1)
    up.step3()
    up_z.send()
    border(2)
    job1.step1()
    border(3)
    down_z.sum()
    middle(g2)
    job1.step2()
    up_z.sum()
    job2 = shard_grads(2, g2)
    middle(g3)
    job2.step1()
    job1.step3()
    send_shard(0, job1)
    down_z.start()
    out_move.wait()
    job3 = shard_grads(3, g3)
    up_z.start()
    middle(z)
    job3.step1()
    job2.step2()
    down_z.spread.step1()
    job0 = shard_grads(0, z)

    def tokens_back(low, size):
        at = slice(low, low + size)
        dn = tn(
            dqkv[:, :, :, at].reshape(shards * 3 * width, size),
            jnp.concatenate([wg[g, : 3 * width, :] for g in range(shards)], axis=0),
        )
        zz, r = norm_stats(x[at, :].astype(F32))
        gain_sum[0:1, :] += jnp.sum(dn * zz, axis=0, keepdims=True)
        dres[at, :] = dres[at, :] + norm_back(dn, zz, r, gain_a[...].reshape(1, D))

    tokens_back(0, BLK // 2)
    job0.step1()
    up_z.spread.step1()
    down_z.spread.step2()
    job3.step2()
    tokens_back(BLK // 2, BLK)
    job2.step3()
    send_shard(1, job2)
    job3.step3()
    send_shard(2, job3)
    up_z.spread.step2()
    tokens_back(BLK // 2 + BLK, BLK // 2)
    move(dres, dtok_to)

    def gain_swap(bit):
        return link.send(gain_sum, gain_got.at[bit], place.near(bit))

    def gain_add(bit, copy):
        copy.wait_recv()
        link.done(copy)
        gain_sum[...] += gain_got[bit]

    def own_sum(lane):
        mine = job0.mine(lane)
        for k in range(1, shards):
            z_copy(k, lane, mine).wait_recv()
        add_rows(mine, *[zk.at[k, lane] for k in range(shards - 1)])

    swapped = gain_swap(0)
    if len(place.bits) == HALVINGS:
        job0.step2(own_sum, r_last)
        gain_add(0, swapped)
        swapped = gain_swap(1)
        down_z.spread.finish()
        up_z.spread.finish()
        move(f_ud.at[0], up_to)
        move(f_ud.at[1], down_to)
        gain_add(1, swapped)
        swapped = gain_swap(2)
        job0.step3_both(r_last, own_spread)
        gain_add(2, swapped)
    else:
        job0.step2()
        gain_add(0, swapped)
        for bit in range(1, len(place.bits)):
            gain_add(bit, gain_swap(bit))
        down_z.spread.finish()
        up_z.spread.finish()
        move(f_ud.at[0], up_to)
        move(f_ud.at[1], down_to)
        job0.step3()
        for lane in range(2):
            own_sum(lane)
            f_own.at[piece_rows(*place.index(lane), lane)][...] = job0.mine(lane)[...]
        own_spread.start()
        own_spread.step1()
    gain_col[z] = gain_sum[...]
    gain_copies = [link.send(gain_sum, gain_col.at[z], column(k)) for k in range(1, shards)]
    own_spread.step2()
    for copy in gain_copies:
        copy.wait_recv()
    gains_out[...] = sum(gain_col[k] for k in range(shards))
    own_spread.finish()
    move(f_own, own_to)

    link.drain()
    for keep, copies in passed:

        @pl.when(keep)
        def _():
            for copy in copies:
                copy.wait_send()

    @pl.when(z < last)
    def _():
        to_next.wait_send()
        for g in range(shards):
            halo_copy(1, g).wait_send()

    @pl.when(z > 0)
    def _():
        to_prev.wait_send()
        for g in range(shards):
            halo_copy(0, g).wait_send()

    for copy in moves[len(own_w + ffn_w) + 1 :]:
        copy.wait()


VM = pl.BlockSpec(memory_space=pltpu.VMEM)
SM = pl.BlockSpec(memory_space=pltpu.SMEM)
ANY = pl.BlockSpec(memory_space=pl.ANY)
COPIES = 224


def S(shape, dtype):
    return jax.ShapeDtypeStruct(shape, dtype)


def layer(dp_size, n, width, *operands):
    pairs = width // (2 * HEAD_DIM)
    step = 8
    more = 0
    while step < dp_size:
        step *= 2
        more += 1
    extra = max(more, 1)
    bits = 3 + more
    V = pltpu.VMEM
    return pl.pallas_call(
        functools.partial(kernel, dp_size, n),
        out_shape=(
            S((ROWS, D), BF), S((ROWS, D), F32), S((8, D), F32), S((D, D), BF), S((D, D), BF), S((D, D), BF),
        ),
        in_specs=[SM, SM, VM, ANY, VM, VM] + [ANY] * 4,
        out_specs=(ANY, ANY, VM, ANY, ANY, ANY),
        scratch_shapes=[
            V((n, D, D), BF),
            V((ROWS, D), BF),
            V((D, D), BF),
            V((D, D), BF),
            V((2, D, D), BF),
            V((D, D), BF),
            V((WIN, D), BF),
            V((2, SLOT, D), BF),
            V((pairs, width + WIDER, 2 * SLOT), BF),
            V((n, width + WIDER, ROWS), BF),
            V((n, width, WIN), BF),
            V((n, width, WIN), BF),
            V((n, WIN + SLOT, width + WIDER), BF),
            V((n, WIN, width + WIDER), BF),
            V((n, SLOTS_DEV, pairs, 2 * SLOT, 2 * SLOT), BF),
            V((n, width, ROWS), F32),
            V((n, width, ROWS), F32),
            V((D, ROWS), BF),
            V((n, width, ROWS), BF),
            V((ROWS, D), BF),
            V((ROWS, D), F32),
            V((n, 3, width, ROWS), BF),
            V((n, width, WIN), F32),
            V((n, width, WIN), F32),
            V((2, n, 2, width, SLOT), BF),
            V((2, n, 2, width, SLOT), BF),
            V((2, D, D), BF),
            V((n, D, D), BF),
            V((n + 2, D // 2, D), BF),
            V((n + 2, 2, 2, LANE, D), BF),
            V((n + 2, 2, LANE, D), BF),
            V((n + 2, extra, 2, LANE, D), BF),
            V((2, 2, LANE, D), BF),
            V((2, n - 1, LANE, D // 2), BF),
            V((n - 1, 2, LANE, D), BF),
            V((8, D), F32),
            V((bits, 8, D), F32),
            V((n, 8, D), F32),
            pltpu.SemaphoreType.DMA((COPIES + 12 * more,)),
            pltpu.SemaphoreType.DMA((COPIES + 12 * more,)),
            pltpu.SemaphoreType.DMA((2, n)),
            pltpu.SemaphoreType.DMA((2, n)),
            pltpu.SemaphoreType.DMA((16,)),
        ],
        compiler_params=pltpu.CompilerParams(
            vmem_limit_bytes=67043328, collective_id=0, has_side_effects=True
        ),
        name="layer",
    )(*operands)


CHUNK = 128


def finish_kernel(width, out, dtok, gains, up, down, own, *refs):
    outs, (out_v, dtok_v, raw, wide, in_sem, out_sem) = refs[:8], refs[8:]
    out_to, dtok_to, gain_a_to, gain_f_to, qkv_to, wo_to, up_to, down_to = outs
    parts = [(up, up_to, i, i) for i in range(0, D, CHUNK)] + [(down, down_to, i, i) for i in range(0, D, CHUNK)]
    size = CHUNK // 2
    small = [(own, qkv_to, i, i) for i in range(0, 3 * width, size)]
    small += [(own, wo_to, 3 * width + i, i) for i in range(0, width, size)]
    jobs = [(a, b, i, j, CHUNK) for a, b, i, j in parts] + [(a, b, i, j, size) for a, b, i, j in small]
    loads, at = [], 0
    for n, (src, _, i, _, rows) in enumerate(jobs):
        copy = pltpu.make_async_copy(src.at[pl.ds(i, rows)], raw.at[pl.ds(at, rows)], in_sem.at[n])
        copy.start()
        loads.append(copy)
        at += rows
    through = []
    for n, (src, mid, dst) in enumerate(((dtok, dtok_v, dtok_to), (out, out_v, out_to))):
        first = pltpu.make_async_copy(src, mid, in_sem.at[len(jobs) + n])
        first.start()
        through.append((first, pltpu.make_async_copy(mid, dst, out_sem.at[len(jobs) + n])))
    gain_a_to[...] = gains[0, :]
    gain_f_to[...] = gains[1, :]
    stores, at = [], 0
    for n, (_, dst, _, j, rows) in enumerate(jobs):
        loads[n].wait()

        @pl.loop(0, rows // 16)
        def _(i):
            rows16 = pl.ds(pl.multiple_of(at + i * 16, 16), 16)
            wide[rows16, :] = raw[rows16, :].astype(F32)

        copy = pltpu.make_async_copy(wide.at[pl.ds(at, rows)], dst.at[pl.ds(j, rows)], out_sem.at[n])
        copy.start()
        stores.append(copy)
        at += rows
    for first, second in through:
        first.wait()
        second.start()
        stores.append(second)
    for copy in stores:
        copy.wait()


def finish(width, *operands):
    V = pltpu.VMEM
    sems = pltpu.SemaphoreType.DMA((2 * D // CHUNK + 2 * D // CHUNK + 2,))
    return pl.pallas_call(
        functools.partial(finish_kernel, width),
        out_shape=(
            S((ROWS, D), BF), S((ROWS, D), F32), S((D,), F32), S((D,), F32),
            S((3 * width, D), F32), S((width, D), F32), S((D, D), F32), S((D, D), F32),
        ),
        in_specs=[ANY, ANY, VM, ANY, ANY, ANY],
        out_specs=(ANY, ANY, VM, VM, ANY, ANY, ANY, ANY),
        scratch_shapes=[V((ROWS, D), BF), V((ROWS, D), F32), V((3 * D, D), BF), V((3 * D, D), F32), sems, sems],
        name="finish",
    )(*operands)


def local(tokens_in, gain_attn, gain_ffn, w_qkv, w_out, w_up, w_down, slot_mol, slot_fill, cotangent):
    n = lax.axis_size("head")
    width = w_out.shape[0]
    results = layer(
        lax.axis_size("dp"), n, width,
        slot_mol, slot_fill, tokens_in, cotangent, gain_attn, gain_ffn,
        w_qkv.transpose(0, 2, 1).reshape(3 * width, D), w_out, w_up, w_down,
    )
    out, dtok, d_gain_a, d_gain_f, d_qkv, d_wo, d_up, d_down = finish(width, *results)
    return (
        out, dtok, d_gain_a, d_gain_f, d_qkv.reshape(3, width, D).transpose(0, 2, 1), d_wo, d_up, d_down,
    )


def solution(mesh):
    return jax.shard_map(
        local,
        mesh=mesh,
        in_specs=(
            P(("dp", "head"), None), P(), P(), P(None, None, "head"), P("head", None), P(), P(),
            P("dp", None), P("dp", None), P(("dp", "head"), None),
        ),
        out_specs=(
            P(("dp", "head"), None), P(("dp", "head"), None), P(), P(), P(None, None, "head"), P("head", None), P(), P(),
        ),
        check_vma=False,
    )
```

time: 160 us -> 141 us (0.88)
  local copies, waits for them, and re-layouts: 9.3 us -> 0 us
  Pallas kernels: 145 us -> 140 us
  other arithmetic: 4.38 us -> 0 us
    pallas_call x1, Pallas kernels: 145 us -> 133 us  [layer(): pl.pallas_call(functools.partial(kernel, dp_size, n), out_shape=(S((ROWS,...]
    pallas_call x0 -> x1, Pallas kernels: none -> 7.59 us  [finish(): pl.pallas_call(functools.partial(finish_kernel, width), out_shape=(S((ROW...]
    slice x3 -> x0, local copies, waits for them, and re-layouts: 3.61 us -> none  [the longest x2 2.28 us: local(): return (out, dtok, gains[0], gains[1], gqkv, own[3 * width:], ud[0], ud[1])]
    squeeze x1 -> x0, local copies, waits for them, and re-layouts: 2.49 us -> none  [local(): return (out, dtok, gains[0], gains[1], gqkv, own[3 * width:], ud[0], ud[1])]
    concatenate x1 -> x0, other arithmetic: 2.36 us -> none  [local(): jnp.concatenate([w_qkv.transpose(0, 2, 1).reshape(3 * width, D), w_out],...]
    unnamed x12 -> x0, local copies, waits for them, and re-layouts: 2.04 us -> none
    convert_element_type x1 -> x0, other arithmetic: 2.02 us -> none  [local(): ud = ud.astype(F32)]
where the time goes in v2:
time: 141 us
  Pallas kernels  140 us (99%)
    pallas_call x1, Pallas kernels, layer(): pl.pallas_call(functools.partial(kernel, dp_size, n), out_shape=(S((ROWS,...  133 us
    pallas_call x1, Pallas kernels, finish(): pl.pallas_call(functools.partial(finish_kernel, width), out_shape=(S((ROW...  7.59 us

profile of v2, /device:TPU:0, one launch (start us, length us, event | category | flops | bytes accessed | tf_op | source)
XLA Modules:
  0.0 141.1 jit_solution(1194903602538821073)
XLA Ops:
  0.6 132.7 %layer.1 = (bf16[512,768]{1,0:T(8,128)(2,1)}, f32[512,768]{1,0:T(8,128)}, f32[8,768]{1,0:T(8,128)}, bf16[768,768]{1,0:T(8,128)(2,1)}, bf16[768,768]{1,0:T(8,128)(2,1)}, /*index=5*/bf16[768,768]{1,0:T(8,128)(2,1)}) custom-call(s32[1,16]{1,0:T(1,128)} %mol.1, s32[1,16]{1,0:T(1,128)} %fill.1, bf16[512,768]{1,0:T(8,128)(2,1)} %x.1, bf16[512,768]{1,0:T(8,128)(2,1)} %cot_in.1, ...), custom_call_target="tpu_custom_call" | custom-call | tf_op jit(solution)/shard_map/layer/pallas_call | solution.py:910
  133.4 7.6 %finish.1 = (bf16[512,768]{1,0:T(8,128)(2,1)}, f32[512,768]{1,0:T(8,128)}, f32[768]{0:T(1024)}, f32[768]{0:T(1024)}, f32[576,768]{1,0:T(8,128)}, /*index=5*/f32[...) custom-call(bf16[512,768]{1,0:T(8,128)(2,1)} %get-tuple-element.22.out, f32[512,768]{1,0:T(8,128)} %get-tuple-element.23.dtok, ...), custom_call_target="tpu_custom_call" | custom-call | tf_op jit(solution)/shard_map/finish/pallas_call | solution.py:1017

commit v3 on v2

--- a/solution.py
+++ b/solution.py
@@ -119,7 +119,7 @@
     return pl.ds(own, SLOT), pl.ds(before, SLOT), pl.ds(after, SLOT), pl.ds(before, SLOT)
 
 
-def attend(g, s, meta, mask, qt, kn, vt, probs, share, mixf, mixt):
+def attend(g, s, meta, mask, qt, kn, vt, probs, share, mixf, mixt, room):
     prev, nxt = meta
     own, before, after, mine = windows(s)
     width = vt.shape[1]
@@ -129,13 +129,23 @@
     ones = jnp.ones((16, 2 * SLOT), BF)
     q = qt[g, :, mine]
     q2 = jnp.concatenate([q, q], axis=1)
-    for p in range(mask.shape[0]):
+    pairs = mask.shape[0]
+    left, right = slice(0, 2 * SLOT), slice(2 * SLOT, 4 * SLOT)
+    tops = [None] * pairs
+
+    def score(p):
         scores = nn(keys, q2 * mask[p])
-        top = jnp.max(scores, axis=0, keepdims=True)
-        ex = jnp.exp(scores - top).astype(BF)
-        probs[g, s, p] = ex
+        room[p, :SLOT, left] = scores[:SLOT]
+        room[p, :SLOT, right] = scores[SLOT:]
+        tops[p] = jnp.max(scores, axis=0, keepdims=True)
+
+    def weigh(p):
+        probs[g, s, p, :SLOT, :] = jnp.exp(room[p, :SLOT, left] - tops[p]).astype(BF)
+        probs[g, s, p, SLOT:, :] = jnp.exp(room[p, :SLOT, right] - tops[p]).astype(BF)
+
+    def mix(p):
         head_rows = slice(2 * HEAD_DIM * p, 2 * HEAD_DIM * (p + 1))
-        both = nn(jnp.concatenate([vals[head_rows, :], ones], axis=0), ex)
+        both = nn(jnp.concatenate([vals[head_rows, :], ones], axis=0), probs[g, s, p])
         part = pair_rows(jnp.broadcast_to(1.0 / both[2 * HEAD_DIM : 2 * HEAD_DIM + 1, :], (2 * HEAD_DIM, 2 * SLOT)))
         mixed = pair_rows(both[: 2 * HEAD_DIM, :]) * part
         share[g, head_rows, mine] = part
@@ -143,8 +153,16 @@
         at = pl.ds(pl.multiple_of(g * width + 2 * HEAD_DIM * p, 16), 2 * HEAD_DIM)
         mixt[at, mine] = mixed.astype(BF)
 
-
-def attend_back(g, s, meta, mask, qt, kt, vn, dmt, probs, share, mixf, dqkv, dkt, dvt, scale):
+    for step in range(pairs + 4):
+        if step < pairs:
+            score(step)
+        if 0 <= step - 2 < pairs:
+            weigh(step - 2)
+        if 0 <= step - 4 < pairs:
+            mix(step - 4)
+
+
+def attend_back(g, s, meta, mask, qt, kt, vn, dmt, probs, share, mixf, dqkv, dkt, dvt, scale, room):
     prev, nxt = meta
     own, before, after, mine = windows(s)
     width = dmt.shape[1]
@@ -158,8 +176,16 @@
     prod = dm.astype(F32) * mixf[g, :, mine]
     line = lax.broadcasted_iota(jnp.int32, (16, 2 * SLOT), 0)
     rest = jnp.zeros((WIDER - 16, 2 * SLOT), BF)
-    for p in range(mask.shape[0]):
-        head_rows = slice(2 * HEAD_DIM * p, 2 * HEAD_DIM * (p + 1))
+    pairs = mask.shape[0]
+    kept = [None] * pairs
+
+    def rows_of(p):
+        return slice(2 * HEAD_DIM * p, 2 * HEAD_DIM * (p + 1))
+
+    def place_of(p):
+        return room.at[pl.ds(p // 3 * 2 * SLOT, 2 * SLOT), pl.ds(p % 3 * 2 * SLOT, 2 * SLOT)]
+
+    def slopes(p):
         mid = 2 * HEAD_DIM * p + HEAD_DIM
         inner = jnp.concatenate(
             [
@@ -172,19 +198,29 @@
         take_off = jnp.where(line == 0, -high, jnp.where(line == 1, high - inner, 0.0)).astype(BF)
         rhs = dm2 * mask[p, :width, :]
         d_probs = nn(vals, jnp.concatenate([rhs, take_off, rest], axis=0))
-        pr = probs[g, s, p]
-        d_scores = pr * d_probs.astype(BF)
+        place_of(p)[...] = probs[g, s, p] * d_probs.astype(BF)
+        kept[p] = nt(rhs[rows_of(p), :], probs[g, s, p])
+
+    def pull(p):
+        head_rows = rows_of(p)
+        d_scores = place_of(p)[...]
         dq = pair_rows(nn(keys[head_rows, :], d_scores)) * scale
         dqkv[g, 0, head_rows, mine] = dq.astype(BF)
         qm = (q2 * mask[p, :width, :])[head_rows, :]
         dk = nt(qm, d_scores)
-        dv = nt(rhs[head_rows, :], pr)
+        dv = kept[p]
         dkt[g, head_rows, own] += dk[:, :SLOT]
         dvt[g, head_rows, own] += dv[:, :SLOT]
         dkt[g, head_rows, before] += fprev * dk[:, SLOT:]
         dvt[g, head_rows, before] += fprev * dv[:, SLOT:]
         dkt[g, head_rows, after] += fnext * dk[:, SLOT:]
         dvt[g, head_rows, after] += fnext * dv[:, SLOT:]
+
+    for step in range(pairs + 2):
+        if step < pairs:
+            slopes(step)
+        if step >= 2:
+            pull(step - 2)
 
 
 SQH = 0.7071067811865476
@@ -304,7 +340,7 @@
                 sent.append(self.link.send(part, self.r1.at[lane, b], p.near(p.order[lane][1])))
             self.copies.append(sent)
 
-    def step2(self, finish=None, r_last=None):
+    def step2(self):
         p = self.place
         old, self.copies = self.copies, []
         for lane in range(2):
@@ -312,18 +348,6 @@
             for b in range(2):
                 self.keep[lane][b].wait_recv()
                 old[lane][b].wait_recv()
-            if finish is not None:
-                for b in range(2):
-                    part = self.g.at[piece_rows(c0, c1, b, lane)]
-                    add_rows(part, self.r0.at[piece_rows(0, c1, b, lane)], self.r1.at[lane, b])
-                finish(lane)
-                self.copies.append(
-                    [
-                        self.link.send(self.g.at[piece_rows(c0, c1, b, lane)], r_last.at[lane, b], p.near(p.order[lane][2]))
-                        for b in range(2)
-                    ]
-                )
-                continue
             part = self.g.at[piece_rows(c0, c1, 1 - c2, lane)]
             add_rows(part, self.r0.at[piece_rows(0, c1, 1 - c2, lane)], self.r1.at[lane, 1 - c2])
             self.copies.append(self.link.send(part, self.r2.at[lane], p.near(p.order[lane][2])))
@@ -344,22 +368,6 @@
                 add_rows(self.mine(lane), self.rx.at[extra - HALVINGS, lane])
 
 
-    def step3_both(self, r_last, spread):
-        p = self.place
-        spread.begin()
-        for lane in range(2):
-            c0, c1, c2 = p.index(lane)
-            for b in range(2):
-                self.copies[lane][b].wait_recv()
-            for b in range(2):
-                rows = piece_rows(c0, c1, b, lane)
-                self.link.done(self.copies[lane][b])
-                add_rows(self.g.at[rows], r_last.at[lane, b])
-                spread.f.at[rows][...] = self.g.at[rows][...]
-            for b in range(2):
-                spread.pass_on(lane, piece_rows(c0, c1, b, lane))
-
-
 class Spread:
     def __init__(self, link, place, f):
         self.link, self.place, self.f = link, place, f
@@ -410,7 +418,7 @@
     out_to, dtok_to, gains_out, up_to, down_to, own_to,
     wg, cot, wu, wd, f_ud, f_own,
     nw, xh, mask, qt, kt, vt, kn, vn, probs, share, mixf, mixt, dmt, dbr, dres,
-    dqkv, dkt, dvt, halo_out, halo_in, g_ud, g_k, r0, r1, r2, rx, r_last, zud, zk,
+    dqkv, dkt, dvt, halo_out, halo_in, g_ud, g_k, r0, r1, r2, rx, zud, zk,
     gain_sum, gain_got, gain_col,
     send_sem, recv_sem, halo_send, halo_recv, load_sem,
 ):
@@ -543,7 +551,7 @@
         @pl.loop(0, (high - low) // step)
         def _(i):
             s = low + i * step
-            attend(g, s, slot_meta(mol, z, s), mask, qt, kn, vt, probs, share, mixf, mixt)
+            attend(g, s, slot_meta(mol, z, s), mask, qt, kn, vt, probs, share, mixf, mixt, dkt)
 
     project(z, [weight(z, c) for c in range(3)], nw, SLOT, ROWS, qt, kt, vt, kn, vn, scale)
     heads_mix(z, 1, SLOTS_DEV - 1)
@@ -651,7 +659,7 @@
 
     def back(g, s):
         attend_back(
-            g, s, slot_meta(mol, z, s), mask, qt, kt, vn, dmt, probs, share, mixf, dqkv, dkt, dvt, scale
+            g, s, slot_meta(mol, z, s), mask, qt, kt, vn, dmt, probs, share, mixf, dqkv, dkt, dvt, scale, f_own
         )
 
     def halo_copy(side, g):
@@ -742,51 +750,43 @@
     up_z, down_z = Column(0), Column(1)
     own_spread = Spread(link, place, f_own)
 
-    upper = (z * 2) // shards
-    turn = [1 + upper, 2 + upper, 3 - 2 * upper]
-    z_slot = link.reserve(2 * (shards - 1))
-
-    def z_copy(k, lane, src):
-        return link.make(src, zk.at[k - 1, lane], column(k), z_slot + 2 * (k - 1) + lane)
-
-    def send_shard(i, job):
-        for lane in range(2):
-            copy = z_copy(turn[i], lane, job.mine(lane))
-            copy.start()
-            link.open.append(copy)
-
-    g1, g2, g3 = (place.across(k) for k in turn)
+    def send_shard(k, job):
+        return [link.send(job.mine(lane), zk.at[k - 1, lane], column(k)) for lane in range(2)]
+
+    g1, g2, g3 = (place.across(k) for k in (3, 2, 1))
     border(0)
     down.step2()
     border(1)
     up.step2()
-    middle(g1)
+    border(2)
     down.step3()
     down_z.send()
-    job1 = shard_grads(1, g1)
+    border(3)
     up.step3()
     up_z.send()
-    border(2)
+    middle(g1)
+    down_z.sum()
+    job1 = shard_grads(1, g1)
+    middle(g2)
     job1.step1()
-    border(3)
-    down_z.sum()
-    middle(g2)
-    job1.step2()
     up_z.sum()
     job2 = shard_grads(2, g2)
+    down_z.start()
     middle(g3)
+    job1.step2()
     job2.step1()
-    job1.step3()
-    send_shard(0, job1)
-    down_z.start()
+    down_z.spread.step1()
     out_move.wait()
     job3 = shard_grads(3, g3)
     up_z.start()
+    job1.step3()
+    z1 = send_shard(3, job1)
     middle(z)
     job3.step1()
     job2.step2()
-    down_z.spread.step1()
     job0 = shard_grads(0, z)
+    down_z.spread.step2()
+    up_z.spread.step1()
 
     def tokens_back(low, size):
         at = slice(low, low + size)
@@ -800,15 +800,14 @@
 
     tokens_back(0, BLK // 2)
     job0.step1()
-    up_z.spread.step1()
-    down_z.spread.step2()
     job3.step2()
+    job2.step3()
+    z2 = send_shard(2, job2)
     tokens_back(BLK // 2, BLK)
-    job2.step3()
-    send_shard(1, job2)
+    up_z.spread.step2()
     job3.step3()
-    send_shard(2, job3)
-    up_z.spread.step2()
+    z3 = send_shard(1, job3)
+    job0.step2()
     tokens_back(BLK // 2 + BLK, BLK // 2)
     move(dres, dtok_to)
 
@@ -820,42 +819,29 @@
         link.done(copy)
         gain_sum[...] += gain_got[bit]
 
-    def own_sum(lane):
+    swapped = gain_swap(0)
+    job0.step3()
+    gain_add(0, swapped)
+    swapped = gain_swap(1)
+    for copy in z1 + z2 + z3:
+        copy.wait_recv()
+    for lane in range(2):
         mine = job0.mine(lane)
-        for k in range(1, shards):
-            z_copy(k, lane, mine).wait_recv()
         add_rows(mine, *[zk.at[k, lane] for k in range(shards - 1)])
-
-    swapped = gain_swap(0)
-    if len(place.bits) == HALVINGS:
-        job0.step2(own_sum, r_last)
-        gain_add(0, swapped)
-        swapped = gain_swap(1)
-        down_z.spread.finish()
-        up_z.spread.finish()
-        move(f_ud.at[0], up_to)
-        move(f_ud.at[1], down_to)
-        gain_add(1, swapped)
-        swapped = gain_swap(2)
-        job0.step3_both(r_last, own_spread)
-        gain_add(2, swapped)
-    else:
-        job0.step2()
-        gain_add(0, swapped)
-        for bit in range(1, len(place.bits)):
-            gain_add(bit, gain_swap(bit))
-        down_z.spread.finish()
-        up_z.spread.finish()
-        move(f_ud.at[0], up_to)
-        move(f_ud.at[1], down_to)
-        job0.step3()
-        for lane in range(2):
-            own_sum(lane)
-            f_own.at[piece_rows(*place.index(lane), lane)][...] = job0.mine(lane)[...]
-        own_spread.start()
-        own_spread.step1()
+        f_own.at[piece_rows(*place.index(lane), lane)][...] = mine[...]
+    own_spread.start()
+    gain_add(1, swapped)
+    swapped = gain_swap(2)
+    down_z.spread.finish()
+    move(f_ud.at[1], down_to)
+    own_spread.step1()
+    gain_add(2, swapped)
+    for bit in range(3, len(place.bits)):
+        gain_add(bit, gain_swap(bit))
     gain_col[z] = gain_sum[...]
     gain_copies = [link.send(gain_sum, gain_col.at[z], column(k)) for k in range(1, shards)]
+    up_z.spread.finish()
+    move(f_ud.at[0], up_to)
     own_spread.step2()
     for copy in gain_copies:
         copy.wait_recv()
@@ -947,7 +933,6 @@
             V((n + 2, 2, 2, LANE, D), BF),
             V((n + 2, 2, LANE, D), BF),
             V((n + 2, extra, 2, LANE, D), BF),
-            V((2, 2, LANE, D), BF),
             V((2, n - 1, LANE, D // 2), BF),
             V((n - 1, 2, LANE, D), BF),
             V((8, D), F32),

time: 141 us -> 127 us (0.901)
  Pallas kernels: 140 us -> 126 us
    pallas_call x1, Pallas kernels: 133 us -> 118 us  [layer(): pl.pallas_call(functools.partial(kernel, dp_size, n), out_shape=(S((ROWS,...]
where the time goes in v3:
time: 127 us; the launch traced here: 126 us
  Pallas kernels  126 us (99%)
    pallas_call x1, Pallas kernels, layer(): pl.pallas_call(functools.partial(kernel, dp_size, n), out_shape=(S((ROWS,...  118 us
    pallas_call x1, Pallas kernels, finish(): pl.pallas_call(functools.partial(finish_kernel, width), out_shape=(S((ROW...  7.59 us

profile of v3, /device:TPU:0, one launch (start us, length us, event | category | flops | bytes accessed | tf_op | source)
XLA Modules:
  0.0 126.5 jit_solution(13928105848451170310)
XLA Ops:
  0.6 118.1 %layer.1 = (bf16[512,768]{1,0:T(8,128)(2,1)}, f32[512,768]{1,0:T(8,128)}, f32[8,768]{1,0:T(8,128)}, bf16[768,768]{1,0:T(8,128)(2,1)}, bf16[768,768]{1,0:T(8,128)(2,1)}, /*index=5*/bf16[768,768]{1,0:T(8,128)(2,1)}) custom-call(s32[1,16]{1,0:T(1,128)} %mol.1, s32[1,16]{1,0:T(1,128)} %fill.1, bf16[512,768]{1,0:T(8,128)(2,1)} %x.1, bf16[512,768]{1,0:T(8,128)(2,1)} %cot_in.1, ...), custom_call_target="tpu_custom_call" | custom-call | tf_op jit(solution)/shard_map/layer/pallas_call | solution.py:896
  118.7 7.6 %finish.1 = (bf16[512,768]{1,0:T(8,128)(2,1)}, f32[512,768]{1,0:T(8,128)}, f32[768]{0:T(1024)}, f32[768]{0:T(1024)}, f32[576,768]{1,0:T(8,128)}, /*index=5*/f32[...) custom-call(bf16[512,768]{1,0:T(8,128)(2,1)} %get-tuple-element.22.out, f32[512,768]{1,0:T(8,128)} %get-tuple-element.23.dtok, ...), custom_call_target="tpu_custom_call" | custom-call | tf_op jit(solution)/shard_map/finish/pallas_call | solution.py:1002

commit v4 on v3

--- a/solution.py
+++ b/solution.py
@@ -554,8 +554,9 @@
             attend(g, s, slot_meta(mol, z, s), mask, qt, kn, vt, probs, share, mixf, mixt, dkt)
 
     project(z, [weight(z, c) for c in range(3)], nw, SLOT, ROWS, qt, kt, vt, kn, vn, scale)
+    pick_up(1)
     heads_mix(z, 1, SLOTS_DEV - 1)
-    pick_up(1)
+    spread[1].step1()
 
     @pl.when(z > 0)
     def _():
@@ -581,53 +582,52 @@
 
     for low in (0, SLOT + ROWS):
         project(z, [None, weight(z, 1), weight(z, 2)], nw, low, SLOT, qt, kt, vt, kn, vn, scale)
-    spread[1].step1()
     pick_up(2)
+    spread[1].step2()
     heads_mix(z, 0, 2 * (SLOTS_DEV - 1), SLOTS_DEV - 1)
+
+    def mix_out(g):
+        at = pl.ds(pl.multiple_of(g * width, 16), width)
+        dres[...] += tn(mixt[at, :], weight(g, 3))
 
     def heads_in(g):
         project(g, [weight(g, c) for c in range(3)], nw, 0, WIN, qt, kt, vt, kn, vn, scale)
 
-    spread[1].step2()
     spread[2].step1()
     pick_up(3)
+    dres[...] = x[...].astype(F32)
+    mix_out(z)
+    for copy in ffn_w:
+        copy.wait()
+    for i in range(ROWS // SLOT):
+        dvt[i, :SLOT, :] = nt(cot[i * SLOT : (i + 1) * SLOT, :], wd[...])
     spread[1].finish()
     heads_in(near_z[0])
     spread[2].step2()
     spread[3].step1()
     heads_mix(near_z[0], 0, SLOTS_DEV)
+    mix_out(near_z[0])
     spread[2].finish()
     spread[3].step2()
     heads_in(near_z[1])
     heads_mix(near_z[1], 0, SLOTS_DEV)
+    mix_out(near_z[1])
     spread[3].finish()
     heads_in(near_z[2])
     heads_mix(near_z[2], 0, SLOTS_DEV)
-
-    mixn = mixt[...].T
-    total = x[...].astype(F32)
-    for g in range(shards):
-        total = total + nn(mixn[:, g * width : (g + 1) * width], weight(g, 3))
-    dres[...] = total
+    mix_out(near_z[2])
 
     gain_sum[...] = jnp.zeros_like(gain_sum)
-
-    @pl.loop(0, ROWS // 64)
-    def _(i):
-        at = pl.ds(pl.multiple_of(i * 64, 64), 64)
-        zz, _ = norm_stats(dres[at, :])
-        nffn[at, :] = (zz * gain_f[...].reshape(1, D)).astype(BF)
-
     BLK = 256
-    for copy in ffn_w:
-        copy.wait()
 
     @pl.loop(0, ROWS // BLK)
     def _(i):
         at = pl.ds(pl.multiple_of(i * BLK, BLK), BLK)
-        u = nn(nffn[at, :], wu[...])
-        c = cot[at, :]
-        dh = nt(c, wd[...])
+        zz, _ = norm_stats(dres[at, :])
+        normed_ffn = (zz * gain_f[...].reshape(1, D)).astype(BF)
+        nffn[at, :] = normed_ffn
+        u = nn(normed_ffn, wu[...])
+        dh = jnp.concatenate([dvt[2 * i, :SLOT, :], dvt[2 * i + 1, :SLOT, :]], axis=0)
         cdf = 0.5 + 0.5 * lax.erf(u * SQH)
         h = (u * cdf).astype(BF)
         hidden[at, :] = h
@@ -635,6 +635,8 @@
         out[at, :] = (dres[at, :] + nn(h, wd[...])).astype(BF)
 
     out_move = move(out, out_to)
+    dkt[...] = jnp.zeros_like(dkt)
+    dvt[...] = jnp.zeros_like(dvt)
     g_ud[1] = tn(hidden[...], cot[...]).astype(BF)
     down = Halve(link, place, g_ud.at[1], *(r.at[shards + 1] for r in (r0, r1, r2, rx)))
     down.start()
@@ -654,8 +656,6 @@
         dbr[at, :] = dr.astype(BF)
 
     up.step1()
-    dkt[...] = jnp.zeros_like(dkt)
-    dvt[...] = jnp.zeros_like(dvt)
 
     def back(g, s):
         attend_back(

time: 127 us -> 125 us (0.984)
  Pallas kernels: 126 us -> 124 us
where the time goes in v4:
time: 125 us
  Pallas kernels  124 us (99%)
    pallas_call x1, Pallas kernels, layer(): pl.pallas_call(functools.partial(kernel, dp_size, n), out_shape=(S((ROWS,...  117 us
    pallas_call x1, Pallas kernels, finish(): pl.pallas_call(functools.partial(finish_kernel, width), out_shape=(S((ROW...  7.59 us

profile of v4, /device:TPU:0, one launch (start us, length us, event | category | flops | bytes accessed | tf_op | source)
XLA Modules:
  0.0 125.2 jit_solution(1352357151901199996)
XLA Ops:
  0.6 116.8 %layer.1 = (bf16[512,768]{1,0:T(8,128)(2,1)}, f32[512,768]{1,0:T(8,128)}, f32[8,768]{1,0:T(8,128)}, bf16[768,768]{1,0:T(8,128)(2,1)}, bf16[768,768]{1,0:T(8,128)(2,1)}, /*index=5*/bf16[768,768]{1,0:T(8,128)(2,1)}) custom-call(s32[1,16]{1,0:T(1,128)} %mol.1, s32[1,16]{1,0:T(1,128)} %fill.1, bf16[512,768]{1,0:T(8,128)(2,1)} %x.1, bf16[512,768]{1,0:T(8,128)(2,1)} %cot_in.1, ...), custom_call_target="tpu_custom_call" | custom-call | tf_op jit(solution)/shard_map/layer/pallas_call | solution.py:896
  117.5 7.6 %finish.1 = (bf16[512,768]{1,0:T(8,128)(2,1)}, f32[512,768]{1,0:T(8,128)}, f32[768]{0:T(1024)}, f32[768]{0:T(1024)}, f32[576,768]{1,0:T(8,128)}, /*index=5*/f32[...) custom-call(bf16[512,768]{1,0:T(8,128)(2,1)} %get-tuple-element.22.out, f32[512,768]{1,0:T(8,128)} %get-tuple-element.23.dtok, ...), custom_call_target="tpu_custom_call" | custom-call | tf_op jit(solution)/shard_map/finish/pallas_call | solution.py:1002

commit v5 on v4

--- a/solution.py
+++ b/solution.py
@@ -962,20 +962,24 @@
     small = [(own, qkv_to, i, i) for i in range(0, 3 * width, size)]
     small += [(own, wo_to, 3 * width + i, i) for i in range(0, width, size)]
     jobs = [(a, b, i, j, CHUNK) for a, b, i, j in parts] + [(a, b, i, j, size) for a, b, i, j in small]
+    through = []
+    for n, (src, mid, dst) in enumerate(((dtok, dtok_v, dtok_to), (out, out_v, out_to))):
+        first = pltpu.make_async_copy(src, mid, in_sem.at[len(jobs) + n])
+        first.start()
+        through.append((first, pltpu.make_async_copy(mid, dst, out_sem.at[len(jobs) + n])))
     loads, at = [], 0
     for n, (src, _, i, _, rows) in enumerate(jobs):
         copy = pltpu.make_async_copy(src.at[pl.ds(i, rows)], raw.at[pl.ds(at, rows)], in_sem.at[n])
         copy.start()
         loads.append(copy)
         at += rows
-    through = []
-    for n, (src, mid, dst) in enumerate(((dtok, dtok_v, dtok_to), (out, out_v, out_to))):
-        first = pltpu.make_async_copy(src, mid, in_sem.at[len(jobs) + n])
-        first.start()
-        through.append((first, pltpu.make_async_copy(mid, dst, out_sem.at[len(jobs) + n])))
     gain_a_to[...] = gains[0, :]
     gain_f_to[...] = gains[1, :]
     stores, at = [], 0
+    for first, second in through:
+        first.wait()
+        second.start()
+        stores.append(second)
     for n, (_, dst, _, j, rows) in enumerate(jobs):
         loads[n].wait()
 
@@ -988,10 +992,6 @@
         copy.start()
         stores.append(copy)
         at += rows
-    for first, second in through:
-        first.wait()
-        second.start()
-        stores.append(second)
     for copy in stores:
         copy.wait()
 

time: 125 us -> 125 us (level)
  no operation moved by 1% of the time
where the time goes in v5:
time: 125 us; the launch traced here: 124 us
  Pallas kernels  124 us (99%)
    pallas_call x1, Pallas kernels, layer(): pl.pallas_call(functools.partial(kernel, dp_size, n), out_shape=(S((ROWS,...  117 us
    pallas_call x1, Pallas kernels, finish(): pl.pallas_call(functools.partial(finish_kernel, width), out_shape=(S((ROW...  6.76 us

profile of v5, /device:TPU:0, one launch (start us, length us, event | category | flops | bytes accessed | tf_op | source)
XLA Modules:
  0.0 124.4 jit_solution(1293632526952674142)
XLA Ops:
  0.6 116.8 %layer.1 = (bf16[512,768]{1,0:T(8,128)(2,1)}, f32[512,768]{1,0:T(8,128)}, f32[8,768]{1,0:T(8,128)}, bf16[768,768]{1,0:T(8,128)(2,1)}, bf16[768,768]{1,0:T(8,128)(2,1)}, /*index=5*/bf16[768,768]{1,0:T(8,128)(2,1)}) custom-call(s32[1,16]{1,0:T(1,128)} %mol.1, s32[1,16]{1,0:T(1,128)} %fill.1, bf16[512,768]{1,0:T(8,128)(2,1)} %x.1, bf16[512,768]{1,0:T(8,128)(2,1)} %cot_in.1, ...), custom_call_target="tpu_custom_call" | custom-call | tf_op jit(solution)/shard_map/layer/pallas_call | solution.py:896
  117.5 6.8 %finish.1 = (bf16[512,768]{1,0:T(8,128)(2,1)}, f32[512,768]{1,0:T(8,128)}, f32[768]{0:T(1024)}, f32[768]{0:T(1024)}, f32[576,768]{1,0:T(8,128)}, /*index=5*/f32[...) custom-call(bf16[512,768]{1,0:T(8,128)(2,1)} %get-tuple-element.22.out, f32[512,768]{1,0:T(8,128)} %get-tuple-element.23.dtok, ...), custom_call_target="tpu_custom_call" | custom-call | tf_op jit(solution)/shard_map/finish/pallas_call | solution.py:1002
